TPU v7x, 256 devices: a whole 4x4x8 slice. The times are simulated.
256 devices in a mesh: dom: 32 (over z, y), member: 8 (over x, core).
Axes of the slice: x: 4, y: 4, z: 8, core: 2. Of those that a mesh axis runs over, the one named last changes fastest.
Arguments:
- state: float32 [64, 3072, 512], P('member', 'dom'), may hold values from -6 to 6
- noise: bfloat16 [8, 64, 3072, 512], P(None, 'member', 'dom'), may hold values from -1.75 to 1.75
- w_local: bfloat16 [512, 512], replicated, may hold values from -0.25 to 0.25
- conn_weight: float32 [16, 3072], P(None, 'dom'), may hold values from -1.75 to 1.75
- conn_index: int32 [16, 3072], P(None, 'dom'), may hold values from 0 to 223, as said below
- boundary: int32 [32, 8], P('dom'), may hold values from 0 to 95, as said below
- send_pos: int32 [32, 32, 4], replicated, may hold values from 0 to 7
- readout: float32 [512], replicated, may hold values from -0.25 to 0.25
- observed: int32 [32, 64], P('dom'), may hold values from 0 to 95, as said below
- obs_value: float32 [32, 64], P('dom'), may hold values from -6 to 6
- obs_var: float32 [32, 64], P('dom'), may hold values from 0.1 to 1
- obs_pert: float32 [64, 32, 64], P('member', 'dom'), may hold values from -6 to 6
Outputs:
- analysis: float32 [64, 3072, 512], P('member', 'dom')
Inputs may be any that keep to these rules, and one draw needn't show every extreme that they name: `conn_index`: each voxel's inputs number 12 rows of its own part (below 96) and 4 received slots; every slot is read by some voxel of its part. Each part's boundary rows are distinct. Each part's observed rows are distinct.
All inputs are finite; a program needn't handle non-finite values.
Results may differ from a plain program's by a relative error of at most 0.025.
Values may be sent and summed in bfloat16 or wider, within the bound.
No kernel may reach another device: no remote copies, remote signals or barrier semaphores. Data moves between devices by JAX's collectives and lax.ppermute only.
A program may use at most 64 MiB of HBM per device.

v0:
```python
import jax
import jax.numpy as jnp
from jax import lax
from jax.sharding import PartitionSpec as P

RELAX_RATE = 0.5


def per_device(
    state,
    noise,
    w_local,
    conn_weight,
    conn_index,
    boundary,
    send_pos,
    readout,
    observed,
    obs_value,
    obs_var,
    obs_pert,
):
    mem_local, vox_local, width = state.shape
    parts_count = lax.axis_size("dom")
    part_index = lax.axis_index("dom")
    slot_count = send_pos.shape[2]
    table_rows = vox_local + parts_count * slot_count
    onehot = conn_index[:, :, None] == jnp.arange(table_rows, dtype=jnp.int32)[None, None, :]
    conn_matrix = jnp.sum(jnp.where(onehot, conn_weight[:, :, None], 0.0), axis=0)
    conn_high = conn_matrix.astype(jnp.bfloat16)
    conn_low = (conn_matrix - conn_high.astype(jnp.float32)).astype(jnp.bfloat16)
    own_sends = lax.dynamic_index_in_dim(send_pos, part_index, 0, keepdims=False)
    current = state
    for step_index in range(noise.shape[0]):
        rate = jnp.tanh(current).astype(jnp.bfloat16)
        send_rows = jnp.take(boundary[0], own_sends.reshape(-1), axis=0)
        outgoing = jnp.take(rate, send_rows, axis=1)
        received = lax.all_to_all(outgoing, "dom", split_axis=1, concat_axis=1, tiled=True)
        table = jnp.concatenate([rate, received], axis=1)
        drive = jnp.einsum("vu,mus->mvs", conn_high, table, preferred_element_type=jnp.float32)
        drive = drive + jnp.einsum(
            "vu,mus->mvs", conn_low, table, preferred_element_type=jnp.float32
        )
        inputs = (rate.astype(jnp.float32) + drive).astype(jnp.bfloat16)
        mixed = jnp.dot(
            inputs.reshape(-1, width), w_local, preferred_element_type=jnp.float32
        ).reshape(current.shape)
        current = (
            (1.0 - RELAX_RATE) * current
            + RELAX_RATE * mixed
            + noise[step_index].astype(jnp.float32)
        )
    picked_obs = jnp.take(current, observed[0], axis=1)
    image_local = jnp.einsum("mos,s->mo", picked_obs, readout, precision=lax.Precision.HIGHEST)
    innov_local = (
        obs_value[0][None, :] + jnp.sqrt(obs_var[0])[None, :] * obs_pert[:, 0, :] - image_local
    )
    image_all, innov_all = (
        lax.all_gather(image_local, "member", axis=0, tiled=True),
        lax.all_gather(innov_local, "member", axis=0, tiled=True),
    )
    members_count = image_all.shape[0]
    anomaly = image_all - jnp.mean(image_all, axis=0, keepdims=True)
    covar = jnp.dot(anomaly.T, anomaly, precision=lax.Precision.HIGHEST) / (
        members_count - 1
    ) + jnp.diag(obs_var[0])
    factor = jnp.linalg.cholesky(covar)
    gain = jax.scipy.linalg.cho_solve((factor, True), innov_all.T).T
    mixing = jnp.dot(gain, anomaly.T, precision=lax.Precision.HIGHEST) / (members_count - 1)
    mixing = mixing - jnp.mean(mixing, axis=1, keepdims=True)
    member_index = lax.axis_index("member")
    flat = current.reshape(mem_local, vox_local * width)
    mine_rows = lax.dynamic_slice_in_dim(mixing, member_index * mem_local, mem_local, 0)
    result = flat + jnp.dot(
        mine_rows,
        lax.all_gather(flat.astype(jnp.bfloat16), "member", axis=0, tiled=True).astype(jnp.float32),
        precision=lax.Precision.HIGHEST,
    )
    return result.reshape(mem_local, vox_local, width)


def solution(mesh):
    in_specs = (
        P("member", "dom", None),
        P(None, "member", "dom", None),
        P(),
        P(None, "dom"),
        P(None, "dom"),
        P("dom", None),
        P(),
        P(),
        P("dom", None),
        P("dom", None),
        P("dom", None),
        P("member", "dom", None),
    )
    out_specs = P("member", "dom", None)
    return jax.shard_map(
        per_device, mesh=mesh, in_specs=in_specs, out_specs=out_specs, check_vma=False
    )
```

profile of v0, /device:TPU:1, one launch (start us, length us, event | category | flops | bytes accessed | tf_op | source)
XLA Modules:
  0.0 413.3 jit_solution(9972842336557962693)
XLA Ops:
  9.1 5.0 %compare_and_fusion = (pred[128]{0:T(512)(128)(4,1)S(1)}, s32[128]{0:T(128)S(1)}) fusion(s32[]{:T(128)} %bitcast.8, s32[]{:T(128)} %bitcast.7, s32[]{:T(128)} %bitcast.6, s32[]{:T(128)} %bitcast.5, s32[]{:T(128)} %bitcast.4, s32[]{:T(128)} %bitcast.3, s32[]{:T(128)} %bitcast.2, s32[]{:T(128)} %bitcast.1, s32[128]{0:T(128)S(1)} %reshape.134), kind=kLoop, calls=%fused_computation.119 | loop fusion | flops 3456 | bytes 1184 | tf_op jit(solution)/shard_map/jit(_take)/and | solution.py:37
  18.0 12.3 %all-to-all-start = ((bf16[8,128,512]{2,0,1:T(8,128)(2,1)}), bf16[8,128,512]{2,0,1:T(8,128)(2,1)}, u32[]{:S(2)}, u32[]{:S(2)}) async-start(bf16[8,128,512]{2,0,1:T(8,128)(2,1)} %select_bitcast_fusion.7), calls=%async_computation | async-start | bytes 2097152 | tf_op jit(solution)/shard_map/all_to_all | solution.py:38
  31.0 25.5 %all-to-all-done = bf16[8,128,512]{2,0,1:T(8,128)(2,1)} async-done(((bf16[8,128,512]{2,0,1:T(8,128)(2,1)}), bf16[8,128,512]{2,0,1:T(8,128)(2,1)}, u32[]{:S(2)}, u32[]{:S(2)}) %all-to-all-start) | async-done | bytes 1048608 | tf_op jit(solution)/shard_map/all_to_all | solution.py:38
  59.6 4.3 %tanh_convert_fusion.6 = (bf16[8,96,512]{2,1,0:T(8,128)(2,1)S(1)}, f32[8,96,512]{2,1,0:T(8,128)}) fusion(bf16[8,8,96,512]{3,2,1,0:T(8,128)(2,1)} %param.17, f32[8,96,512]{2,1,0:T(8,128)} %param.16, bf16[512,512]{1,0:T(8,128)(2,1)S(1)} %copy-done, f32[8,512,96]{1,2,0:T(8,128)} %fusion.15, bf16[8,96,512]{2,1,0:T(8,128)(2,1)S(1)} %tanh_convert_fusion.7, ...), kind=kOutput, calls=%fused_computation.48 | convolution fusion | flops 586022912 | bytes 9486336 | tf_op jit(solution)/shard_map/dot_general | solution.py:45
  65.3 31.6 %all_to_all.40 = bf16[8,128,512]{2,0,1:T(8,128)(2,1)S(1)} all-to-all(bf16[8,128,512]{2,0,1:T(8,128)(2,1)S(1)} %select_bitcast_fusion.6), channel_id=1, replica_groups=mesh['dom'=32,'member'=8] {'dom'}, dimensions={1} | all-to-all | bytes 2097152 | tf_op jit(solution)/shard_map/all_to_all | solution.py:38
  98.8 4.3 %tanh_convert_fusion.5 = (bf16[8,96,512]{2,1,0:T(8,128)(2,1)S(1)}, f32[8,96,512]{2,1,0:T(8,128)}) fusion(bf16[8,8,96,512]{3,2,1,0:T(8,128)(2,1)} %param.17, f32[8,96,512]{2,1,0:T(8,128)} %get-tuple-element.20, bf16[512,512]{1,0:T(8,128)(2,1)S(1)} %copy-done, f32[8,512,96]{1,2,0:T(8,128)} %fusion.14, bf16[8,96,512]{2,1,0:T(8,128)(2,1)S(1)} %get-tuple-element.19, ...), kind=kOutput, calls=%fused_computation.47 | convolution fusion | flops 586022912 | bytes 9486336 | tf_op jit(solution)/shard_map/dot_general | solution.py:45
  104.5 31.3 %all_to_all.41 = bf16[8,128,512]{2,0,1:T(8,128)(2,1)S(1)} all-to-all(bf16[8,128,512]{2,0,1:T(8,128)(2,1)S(1)} %select_bitcast_fusion.5), channel_id=1, replica_groups=mesh['dom'=32,'member'=8] {'dom'}, dimensions={1} | all-to-all | bytes 2097152 | tf_op jit(solution)/shard_map/all_to_all | solution.py:38
  137.7 4.3 %tanh_convert_fusion.4 = (bf16[8,96,512]{2,1,0:T(8,128)(2,1)S(1)}, f32[8,96,512]{2,1,0:T(8,128)}) fusion(bf16[8,8,96,512]{3,2,1,0:T(8,128)(2,1)} %param.17, f32[8,96,512]{2,1,0:T(8,128)} %get-tuple-element.22, bf16[512,512]{1,0:T(8,128)(2,1)S(1)} %copy-done, f32[8,512,96]{1,2,0:T(8,128)} %fusion.13, bf16[8,96,512]{2,1,0:T(8,128)(2,1)S(1)} %get-tuple-element.21, ...), kind=kOutput, calls=%fused_computation.46 | convolution fusion | flops 586022912 | bytes 9486336 | tf_op jit(solution)/shard_map/dot_general | solution.py:45
  143.4 31.8 %all_to_all.42 = bf16[8,128,512]{2,0,1:T(8,128)(2,1)S(1)} all-to-all(bf16[8,128,512]{2,0,1:T(8,128)(2,1)S(1)} %select_bitcast_fusion.4), channel_id=1, replica_groups=mesh['dom'=32,'member'=8] {'dom'}, dimensions={1} | all-to-all | bytes 2097152 | tf_op jit(solution)/shard_map/all_to_all | solution.py:38
  177.2 4.3 %tanh_convert_fusion.3 = (bf16[8,96,512]{2,1,0:T(8,128)(2,1)S(1)}, f32[8,96,512]{2,1,0:T(8,128)}) fusion(bf16[8,8,96,512]{3,2,1,0:T(8,128)(2,1)} %param.17, f32[8,96,512]{2,1,0:T(8,128)} %get-tuple-element.24, bf16[512,512]{1,0:T(8,128)(2,1)S(1)} %copy-done, f32[8,512,96]{1,2,0:T(8,128)} %fusion.12, bf16[8,96,512]{2,1,0:T(8,128)(2,1)S(1)} %get-tuple-element.23, ...), kind=kOutput, calls=%fused_computation.45 | convolution fusion | flops 586022912 | bytes 9486336 | tf_op jit(solution)/shard_map/dot_general | solution.py:45
  182.9 31.7 %all_to_all.43 = bf16[8,128,512]{2,0,1:T(8,128)(2,1)S(1)} all-to-all(bf16[8,128,512]{2,0,1:T(8,128)(2,1)S(1)} %select_bitcast_fusion.3), channel_id=1, replica_groups=mesh['dom'=32,'member'=8] {'dom'}, dimensions={1} | all-to-all | bytes 2097152 | tf_op jit(solution)/shard_map/all_to_all | solution.py:38
  216.5 4.3 %tanh_convert_fusion.2 = (bf16[8,96,512]{2,1,0:T(8,128)(2,1)S(1)}, f32[8,96,512]{2,1,0:T(8,128)}) fusion(bf16[8,8,96,512]{3,2,1,0:T(8,128)(2,1)} %param.17, f32[8,96,512]{2,1,0:T(8,128)} %get-tuple-element.26, bf16[512,512]{1,0:T(8,128)(2,1)S(1)} %copy-done, f32[8,512,96]{1,2,0:T(8,128)} %fusion.11, bf16[8,96,512]{2,1,0:T(8,128)(2,1)S(1)} %get-tuple-element.25, ...), kind=kOutput, calls=%fused_computation.44 | convolution fusion | flops 586022912 | bytes 9486336 | tf_op jit(solution)/shard_map/dot_general | solution.py:45
  222.2 31.8 %all_to_all.44 = bf16[8,128,512]{2,0,1:T(8,128)(2,1)S(1)} all-to-all(bf16[8,128,512]{2,0,1:T(8,128)(2,1)S(1)} %select_bitcast_fusion.2), channel_id=1, replica_groups=mesh['dom'=32,'member'=8] {'dom'}, dimensions={1} | all-to-all | bytes 2097152 | tf_op jit(solution)/shard_map/all_to_all | solution.py:38
  255.9 4.3 %tanh_convert_fusion.1 = (bf16[8,96,512]{2,1,0:T(8,128)(2,1)S(1)}, f32[8,96,512]{2,1,0:T(8,128)}) fusion(bf16[8,8,96,512]{3,2,1,0:T(8,128)(2,1)} %param.17, f32[8,96,512]{2,1,0:T(8,128)} %get-tuple-element.28, bf16[512,512]{1,0:T(8,128)(2,1)S(1)} %copy-done, f32[8,512,96]{1,2,0:T(8,128)} %fusion.10, bf16[8,96,512]{2,1,0:T(8,128)(2,1)S(1)} %get-tuple-element.27, ...), kind=kOutput, calls=%fused_computation.43 | convolution fusion | flops 586022912 | bytes 9486336 | tf_op jit(solution)/shard_map/dot_general | solution.py:45
  261.6 31.9 %all_to_all.45 = bf16[8,128,512]{2,0,1:T(8,128)(2,1)S(1)} all-to-all(bf16[8,128,512]{2,0,1:T(8,128)(2,1)S(1)} %select_bitcast_fusion.1), channel_id=1, replica_groups=mesh['dom'=32,'member'=8] {'dom'}, dimensions={1} | all-to-all | bytes 2097152 | tf_op jit(solution)/shard_map/all_to_all | solution.py:38
  295.4 4.3 %tanh_convert_fusion = (bf16[8,96,512]{2,1,0:T(8,128)(2,1)S(1)}, f32[8,96,512]{2,1,0:T(8,128)}) fusion(bf16[8,8,96,512]{3,2,1,0:T(8,128)(2,1)} %param.17, f32[8,96,512]{2,1,0:T(8,128)} %get-tuple-element.30, bf16[512,512]{1,0:T(8,128)(2,1)S(1)} %copy-done, f32[8,512,96]{1,2,0:T(8,128)} %fusion.9, bf16[8,96,512]{2,1,0:T(8,128)(2,1)S(1)} %get-tuple-element.29, ...), kind=kOutput, calls=%fused_computation.42 | convolution fusion | flops 586022912 | bytes 9486336 | tf_op jit(solution)/shard_map/dot_general | solution.py:45
  301.1 32.3 %all_to_all.46 = bf16[8,128,512]{2,0,1:T(8,128)(2,1)S(1)} all-to-all(bf16[8,128,512]{2,0,1:T(8,128)(2,1)S(1)} %select_bitcast_fusion), channel_id=1, replica_groups=mesh['dom'=32,'member'=8] {'dom'}, dimensions={1} | all-to-all | bytes 2097152 | tf_op jit(solution)/shard_map/all_to_all | solution.py:38
  335.3 4.2 %convert_add_fusion = f32[8,96,512]{2,1,0:T(8,128)} fusion(f32[8,96,512]{2,1,0:T(8,128)} %get-tuple-element.32, f32[8,512,96]{1,2,0:T(8,128)} %fusion.8, bf16[8,96,512]{2,1,0:T(8,128)(2,1)S(1)} %get-tuple-element.31, bf16[96,224,1]{1,0,2:T(8,128)(2,1)S(1)} %get-tuple-element.6, bf16[8,128,512]{2,1,0:T(8,128)(2,1)S(1)} %copy.78, ...), kind=kOutput, calls=%fused_computation.18 | convolution fusion | flops 585629696 | bytes 8699904 | tf_op jit(solution)/shard_map/dot_general | solution.py:45
  348.5 7.1 %fusion.16 = f32[1,8,64]{1,0,2:T(1,128)S(1)} fusion(f32[512,1,1]{0,1,2:T(1,128)S(1)} %bitcast.214, f32[64,8,512]{2,1,0:T(8,128)S(1)} %gather_fusion, pred[64]{0:T(512)(128)(4,1)S(1)} %compare_and_fusion.1), kind=kOutput, calls=%fused_computation.62 | convolution fusion | flops 3407872 | bytes 1052736 | tf_op jit(solution)/shard_map/mos,s->mo/dot_general | solution.py:54
  355.7 17.5 %all_gather.9 = f32[64,64]{1,0:T(8,128)S(1)} all-gather(f32[8,64]{1,0:T(8,128)S(1)} %bitcast.211), channel_id=1, replica_groups=mesh['dom'=32,'member'=8] {'member'}, dimensions={0}, use_global_device_ids=true | all-gather | bytes 18432 | tf_op jit(solution)/shard_map/all_gather | solution.py:59
  373.6 5.9 %cholesky.16 = f32[64,64]{1,0:T(8,128)S(1)} custom-call(f32[64,64]{1,0:T(8,128)S(1)} %fusion.44), custom_call_target="Cholesky" | custom-call | tf_op jit(solution)/shard_map/jit(cholesky)/cholesky | solution.py:67
  380.8 4.9 %custom-call.10 = f32[1,64,64]{1,2,0:T(8,128)S(1)} custom-call(f32[1,64,64]{2,1,0:T(8,128)S(1)} %fusion.38), custom_call_target="InvertDiagBlocksLowerTriangular" | custom-call | tf_op jit(solution)/shard_map/jit(_cho_solve)/triangular_solve | solution.py:68
  385.7 13.2 %all_gather.10 = f32[64,64]{1,0:T(8,128)S(1)} all-gather(f32[8,64]{1,0:T(8,128)S(1)} %add_subtract_fusion), channel_id=1, replica_groups=mesh['dom'=32,'member'=8] {'member'}, dimensions={0}, use_global_device_ids=true | all-gather | bytes 18432 | tf_op jit(solution)/shard_map/all_gather | solution.py:60
  399.6 4.9 %convolution_add_fusion = f32[8,49152]{1,0:T(8,128)S(1)} fusion(f32[8,49152]{1,0:T(8,128)S(1)} %bitcast.208, bf16[64,49152]{1,0:T(8,128)(2,1)} %all-gather.2.cloned.1.call-done, f32[64,64]{0,1:T(8,128)S(1)} %get-tuple-element.34, s32[]{:T(128)S(6)} %select_n.64, f32[8]{0:T(128)S(1)} %dynamic-slice), kind=kOutput, calls=%fused_computation.9 | convolution fusion | flops 302383616 | bytes 9453604 | tf_op jit(solution)/shard_map/dot_general | solution.py:74
  (93 shorter events, 46.9 us)
Async XLA Ops:
  6.5 53.1 %copy-start = (bf16[512,512]{1,0:T(8,128)(2,1)S(1)}, bf16[512,512]{1,0:T(8,128)(2,1)}, u32[]{:S(2)}) copy-start(bf16[512,512]{1,0:T(8,128)(2,1)} %param.18) | copy-start | bytes 1572868
  14.1 2.1 copy-start.1
  18.0 12.3 %copy-start.2 = (f32[16,96]{1,0:T(8,128)S(1)}, f32[16,96]{1,0:T(8,128)}, u32[]{:S(2)}) copy-start(f32[16,96]{1,0:T(8,128)} %param.19) | copy-start | bytes 18436
  18.0 12.4 %copy-start.3 = (s32[16,96]{1,0:T(8,128)S(1)}, s32[16,96]{1,0:T(8,128)}, u32[]{:S(2)}) copy-start(s32[16,96]{1,0:T(8,128)} %param.20) | copy-start | bytes 18436
  18.0 38.5 %all-to-all-start = ((bf16[8,128,512]{2,0,1:T(8,128)(2,1)}), bf16[8,128,512]{2,0,1:T(8,128)(2,1)}, u32[]{:S(2)}, u32[]{:S(2)}) async-start(bf16[8,128,512]{2,0,1:T(8,128)(2,1)} %select_bitcast_fusion.7), calls=%async_computation | async-start | bytes 2097152 | tf_op jit(solution)/shard_map/all_to_all | solution.py:38
  30.3 369.2 %all-gather.2.cloned.1.call-start = ((), (), s32[]{:S(2)}) async-start(), calls=%async_computation.8 | async-start | bytes 7077888 | tf_op jit(solution)/shard_map/all_gather | solution.py:76
  341.8 1.1 copy-start.8
  341.8 1.2 copy-start.6
  346.4 2.1 copy-start.5
  346.4 39.2 %copy-start.4 = (f32[8,1,64]{2,1,0:T(1,128)S(1)}, f32[8,1,64]{2,1,0:T(1,128)}, u32[]{:S(2)}) copy-start(f32[8,1,64]{2,1,0:T(1,128)} %param.27) | copy-start | bytes 6148
  346.4 39.2 %copy-start.7 = (f32[1,64]{1,0:T(1,128)S(1)}, f32[1,64]{1,0:T(1,128)}, u32[]{:S(2)}) copy-start(f32[1,64]{1,0:T(1,128)} %param.25) | copy-start | bytes 772
Sparse Core Ops, SparseCore 0:
  343.0 44.4 all-gather.1
where the time goes:
time: 414 us; the launch traced here: 413 us
  blocking collectives  253 us (61%)
  matrix products  59.6 us (14%)
  local copies, waits for them, and re-layouts  25.9 us (6%)
  waiting for transfers between devices  25.5 us (6%)
  other arithmetic  23.1 us (6%)
  between operations  13.8 us (3%)
  starting transfers between devices  12.3 us (3%)
    all_to_all x7, blocking collectives, per_device(): lax.all_to_all(outgoing, 'dom', split_axis=1, concat_axis=1, tiled=True)  222 us
    dot_general x8, matrix products, per_device(): jnp.dot(inputs.reshape(-1, width), w_local, preferred_element_type=jnp.fl...  34.2 us
    all_to_all x1, waiting for transfers between devices, per_device(): lax.all_to_all(outgoing, 'dom', split_axis=1, concat_axis=1, tiled=True)  25.5 us
    all_gather x1, blocking collectives, per_device(): lax.all_gather(image_local, 'member', axis=0, tiled=True)  17.5 us
    all_gather x1, blocking collectives, per_device(): lax.all_gather(innov_local, 'member', axis=0, tiled=True)  13.2 us
    dot_general x8, matrix products, per_device(): jnp.einsum('vu,mus->mvs', conn_high, table, preferred_element_type=jnp.fl...  12.7 us
    all_to_all x1, starting transfers between devices, per_device(): lax.all_to_all(outgoing, 'dom', split_axis=1, concat_axis=1, tiled=True)  12.3 us
  transfers between devices with their start and end apart: 2, of which 1 were waited for; matrix products, arithmetic and copies ran while one was open for 6% of the time, Pallas kernels for 0%

commit v1 on v0

v1 whole, which is shorter than its diff:
```python
import functools

import jax
import jax.numpy as jnp
from jax import lax
from jax.experimental import pallas as pl
from jax.experimental.pallas import tpu as pltpu
from jax.sharding import Mesh, PartitionSpec as P

STATE = 512
VOX = 96
STEPS = 8
BND = 8
OBS = 64
KIN = 16
HALO = 128
PARTS = 8
RING = 4
ROWS = PARTS * BND
AUX = 16
TAIL = 8
CHUNK = 48
MEMBERS = 64
BF = jnp.bfloat16
F32 = jnp.float32
HIGH = lax.Precision.HIGHEST


def iota(shape, axis):
    return lax.broadcasted_iota(jnp.int32, shape, axis)


def dot(a, b):
    return jnp.dot(a, b, preferred_element_type=F32)


def pieces(value):
    high = value.astype(BF).astype(F32)
    rest = value - high
    middle = rest.astype(BF).astype(F32)
    return high, middle, rest - middle


def stack_rows(rows, shape):
    row = iota(shape, 0)
    total = jnp.zeros(shape, F32)
    for place, value in enumerate(rows):
        total = jnp.where(row == place, jnp.broadcast_to(value, shape), total)
    return total


def chosen_rows(bound):
    eye = iota((AUX, BND), 0) == iota((AUX, BND), 1)
    column = jnp.sum(jnp.where(eye, bound.astype(F32), 0.0), axis=1, keepdims=True)
    shape = (AUX, 128)
    match = (iota(shape, 1).astype(F32) == column) & (iota(shape, 0) < BND)
    return jnp.where(match, 1.0, 0.0).astype(BF)


def prep_body(state, weight, index, bound, observed, value, var, pert, slab):
    chosen = chosen_rows(bound[...])
    for j in range(2):
        rate = jnp.tanh(state[j]).astype(BF)
        slab[j, 0:VOX, :] = rate
        slab[j, VOX : VOX + AUX, :] = jnp.zeros((AUX, STATE), BF)
        slab[j, VOX : VOX + AUX, 0:VOX] = weight[...].astype(BF)
        slab[j, VOX : VOX + AUX, 128 : 128 + VOX] = index[...].astype(F32).astype(BF)
        shifted = value[...] + jnp.sqrt(var[...]) * pert[j]
        info = (observed[...].astype(F32),) + pieces(shifted)
        slab[j, VOX : VOX + AUX, 256 : 256 + OBS] = stack_rows(info, (AUX, OBS)).astype(BF)
        slab[j, VOX : VOX + AUX, 384:512] = chosen
        slab[j, VOX + AUX : VOX + AUX + BND, :] = dot(chosen[:, 0:VOX], rate)[0:BND].astype(BF)


SMALL = pltpu.CompilerParams(vmem_limit_bytes=20 * 2**20)


def whole(*shape):
    return pl.BlockSpec(shape, lambda q: (0,) * len(shape))


def prep(state, weight, index, bound, observed, value, var, pert):
    return pl.pallas_call(
        prep_body,
        grid=(PARTS // 2,),
        in_specs=[
            pl.BlockSpec((2, VOX, STATE), lambda j: (j, 0, 0)),
            whole(KIN, VOX),
            whole(KIN, VOX),
            whole(1, BND),
            whole(1, OBS),
            whole(1, OBS),
            whole(1, OBS),
            pl.BlockSpec((2, 1, OBS), lambda j: (j, 0, 0)),
        ],
        out_specs=pl.BlockSpec((2, VOX + AUX + BND, STATE), lambda j: (j, 0, 0)),
        out_shape=jax.ShapeDtypeStruct((PARTS, VOX + AUX + BND, STATE), BF),
        name="prep",
        compiler_params=SMALL,
    )(state, weight, index, bound, observed, value, var, pert)


def pack_body(state, noise, bound, first, *packed):
    chosen = chosen_rows(bound[...])[:, 0:VOX]
    start = (0.5 * state[0] + noise[0, 0].astype(F32)).astype(BF)
    first[0, 0:VOX, :] = start
    for t in range(STEPS):
        rows = start if t == 0 else noise[t, 0]
        first[0, VOX + t * BND : VOX + (t + 1) * BND, :] = dot(chosen, rows)[0:BND].astype(BF)
    for steps, out in zip(BATCHES, packed):
        for place, t in enumerate(steps):
            out[0, place] = noise[t, 0]


BATCHES = ((1,), (2, 3), (4, 5), (6, 7))


def pack(state, noise, bound):
    sizes = [len(steps) for steps in BATCHES]
    return pl.pallas_call(
        pack_body,
        grid=(PARTS,),
        in_specs=[
            pl.BlockSpec((1, VOX, STATE), lambda j: (j, 0, 0)),
            pl.BlockSpec((STEPS, 1, VOX, STATE), lambda j: (0, j, 0, 0)),
            whole(1, BND),
        ],
        out_specs=[pl.BlockSpec((1, VOX + STEPS * BND, STATE), lambda j: (j, 0, 0))]
        + [pl.BlockSpec((1, n, VOX, STATE), lambda j: (j, 0, 0, 0)) for n in sizes],
        out_shape=[jax.ShapeDtypeStruct((PARTS, VOX + STEPS * BND, STATE), BF)]
        + [jax.ShapeDtypeStruct((PARTS, n, VOX, STATE), BF) for n in sizes],
        name="pack",
        compiler_params=SMALL,
        cost_estimate=pl.CostEstimate(flops=10**9, bytes_accessed=14 * 10**6, transcendentals=0),
    )(state, noise, bound)


def tables_body(slab, colmap, own, halo, pick, ahead, start):
    weight = slab[0, VOX : VOX + AUX, 0:128].astype(F32)
    index = slab[0, VOX : VOX + AUX, 128:256].astype(F32)
    row = iota((256, 128), 0).astype(F32)
    spread = jnp.zeros((256, 128), F32)
    for k in range(KIN):
        spread = spread + jnp.where(row == index[k : k + 1, :], weight[k : k + 1, :], 0.0)
    local = jnp.transpose(spread[0:128, :])[0:VOX, :]
    slots = jnp.transpose(spread[VOX : VOX + HALO, :])[0:VOX, :].astype(BF)
    place = (iota((RING * ROWS, HALO), 0) == colmap[0]).astype(F32).astype(BF)
    far = lax.dot_general(slots, place, (((1,), (1,)), ((), ())), preferred_element_type=F32).astype(BF)
    chosen = slab[0, VOX : VOX + AUX, 384:512][:, 0:VOX]
    own_matrix = local[:, 0:VOX].astype(BF)
    own[0] = own_matrix
    halo[0] = far
    chosen_own = dot(chosen, own_matrix)
    both = jnp.concatenate([chosen.astype(F32)[0:BND], chosen_own[0:BND]], axis=0).astype(BF)
    pick[0] = both
    ahead[...] = dot(chosen, far)[0:BND].astype(BF)
    found = dot(both, slab[0, 0:VOX, :])
    start[...] = found[0:BND] + found[BND : 2 * BND]


def tables(slab, colmap):
    return pl.pallas_call(
        tables_body,
        grid=(PARTS,),
        in_specs=[
            pl.BlockSpec((1, VOX + AUX, STATE), lambda q: (q, 0, 0)),
            pl.BlockSpec((1, 1, HALO), lambda q: (q, 0, 0)),
        ],
        out_specs=[
            pl.BlockSpec((1, VOX, VOX), lambda q: (q, 0, 0)),
            pl.BlockSpec((1, VOX, RING * ROWS), lambda q: (q, 0, 0)),
            pl.BlockSpec((1, 2 * BND, VOX), lambda q: (q, 0, 0)),
            pl.BlockSpec((BND, RING * ROWS), lambda q: (q, 0)),
            pl.BlockSpec((BND, STATE), lambda q: (q, 0)),
        ],
        out_shape=[
            jax.ShapeDtypeStruct((PARTS, VOX, VOX), BF),
            jax.ShapeDtypeStruct((PARTS, VOX, RING * ROWS), BF),
            jax.ShapeDtypeStruct((PARTS, 2 * BND, VOX), BF),
            jax.ShapeDtypeStruct((ROWS, RING * ROWS), BF),
            jax.ShapeDtypeStruct((ROWS, STATE), F32),
        ],
        name="tables",
        compiler_params=SMALL,
        cost_estimate=pl.CostEstimate(flops=10**9, bytes_accessed=10**7, transcendentals=0),
    )(slab, colmap)


def edge_body(begin, ahead, w, noise, r0, r1, r2, r3, *refs):
    current, (rate_out, current_out) = refs[:-2], refs[-2:]
    table = jnp.concatenate([r0[...], r1[...], r2[...], r3[...]], axis=0)
    inputs = (begin[...] + dot(ahead[...], table)).astype(BF)
    value = 0.5 * dot(inputs, w[...]) + noise[...].astype(F32).reshape(ROWS, STATE)
    if current:
        value = value + 0.5 * current[0][...]
    current_out[...] = value
    rate_out[...] = jnp.tanh(value).astype(BF)


def edge(t, begin, ahead, w, first, table, current):
    more = [] if current is None else [current]
    return pl.pallas_call(
        edge_body,
        grid=(1,),
        in_specs=[
            whole(ROWS, STATE),
            whole(ROWS, RING * ROWS),
            whole(STATE, STATE),
            pl.BlockSpec((PARTS, BND, STATE), lambda q: (0, VOX // BND + t, 0)),
        ]
        + [whole(ROWS, STATE)] * (RING + len(more)),
        out_specs=[whole(ROWS, STATE), whole(ROWS, STATE)],
        out_shape=[
            jax.ShapeDtypeStruct((ROWS, STATE), BF),
            jax.ShapeDtypeStruct((ROWS, STATE), F32),
        ],
        name="edge",
        compiler_params=SMALL,
        cost_estimate=pl.CostEstimate(flops=10**8, bytes_accessed=10**6, transcendentals=0),
    )(begin, ahead, w, first, *table, *more)


GROUP = 4


def advance(rate, own, halo, w, noise, current, table):
    mine = jnp.concatenate([dot(own[i], rate[i]) for i in range(GROUP)], axis=0)
    matrix = jnp.concatenate([halo[i] for i in range(GROUP)], axis=0)
    far = dot(matrix, jnp.concatenate([r[...] for r in table], axis=0))
    inputs = rate[...].astype(F32).reshape(GROUP * VOX, STATE) + mine + far
    mixed = dot(inputs.astype(BF), w[...])
    value = 0.5 * mixed + noise[...].astype(F32).reshape(GROUP * VOX, STATE)
    if current is not None:
        value = value + 0.5 * current[...].reshape(GROUP * VOX, STATE)
    return value


def step_body(has_current, *refs):
    rate, own, halo, pick, w, noise = refs[:6]
    refs = refs[6:]
    current = None
    if has_current:
        current, refs = refs[0], refs[1:]
    table, (current_out, rate_out, begin_out) = refs[:RING], refs[RING:]
    value = advance(rate, own, halo, w, noise, current, table)
    fresh = jnp.tanh(value).astype(BF)
    current_out[...] = value.reshape(GROUP, VOX, STATE)
    rate_out[...] = fresh.reshape(GROUP, VOX, STATE)
    for i in range(GROUP):
        found = dot(pick[i], fresh[i * VOX : (i + 1) * VOX])
        begin_out[i * BND : (i + 1) * BND, :] = found[0:BND] + found[BND : 2 * BND]


def common_specs(has_current, with_pick, place):
    part = lambda *shape: pl.BlockSpec((GROUP,) + shape, lambda q: (q, 0, 0))
    kick = part(VOX, STATE)
    if place is not None:
        kick = pl.BlockSpec((GROUP, 1, VOX, STATE), lambda q: (q, place, 0, 0))
    specs = [part(VOX, STATE), part(VOX, VOX), part(VOX, RING * ROWS)]
    if with_pick:
        specs.append(part(2 * BND, VOX))
    specs += [whole(STATE, STATE), kick]
    if has_current:
        specs.append(part(VOX, STATE))
    specs += [whole(ROWS, STATE)] * RING
    return specs


STEP_COST = pl.CostEstimate(flops=2 * 10**9, bytes_accessed=6 * 10**6, transcendentals=4 * 10**5)


def step(rate, own, halo, pick, w, noise, place, current, table):
    args = [rate, own, halo, pick, w, noise] + ([] if current is None else [current]) + list(table)
    return pl.pallas_call(
        functools.partial(step_body, current is not None),
        grid=(PARTS // GROUP,),
        in_specs=common_specs(current is not None, True, place),
        out_specs=[
            pl.BlockSpec((GROUP, VOX, STATE), lambda q: (q, 0, 0)),
            pl.BlockSpec((GROUP, VOX, STATE), lambda q: (q, 0, 0)),
            pl.BlockSpec((GROUP * BND, STATE), lambda q: (q, 0)),
        ],
        out_shape=[
            jax.ShapeDtypeStruct((PARTS, VOX, STATE), F32),
            jax.ShapeDtypeStruct((PARTS, VOX, STATE), BF),
            jax.ShapeDtypeStruct((ROWS, STATE), F32),
        ],
        name="step",
        compiler_params=SMALL,
        cost_estimate=STEP_COST,
    )(*args)


def last_body(rate, own, halo, w, noise, current, r0, r1, r2, r3, extra, readout, out):
    value = advance(rate, own, halo, w, noise, current, (r0, r1, r2, r3))
    weighted = value * readout[...]
    for i in range(GROUP):
        image_rows = jnp.sum(weighted[i * VOX : (i + 1) * VOX], axis=1, keepdims=True)
        info = extra[i].astype(F32)
        observed = info[0:1, 0:OBS]
        shifted = info[1:2, 0:OBS] + info[2:3, 0:OBS] + info[3:4, 0:OBS]
        seen = iota((VOX, OBS), 0).astype(F32) == observed
        image = jnp.sum(jnp.where(seen, image_rows, 0.0), axis=0, keepdims=True)
        image_block = stack_rows(pieces(image), (TAIL, OBS)).astype(BF)
        innov_block = stack_rows(pieces(shifted - image), (TAIL, OBS)).astype(BF)
        for c in range(8):
            high, quarter = divmod(c, 4)
            begin = i * VOX + high * CHUNK
            out[i * 8 + c, 0:CHUNK, :] = value[
                begin : begin + CHUNK, quarter * 128 : (quarter + 1) * 128
            ].astype(BF)
            out[i * 8 + c, CHUNK : CHUNK + TAIL, 0:OBS] = image_block
            out[i * 8 + c, CHUNK : CHUNK + TAIL, OBS : 2 * OBS] = innov_block


def last(rate, own, halo, w, noise, place, current, table, slab, readout):
    return pl.pallas_call(
        last_body,
        grid=(PARTS // GROUP,),
        in_specs=common_specs(True, False, place)
        + [
            pl.BlockSpec((GROUP, AUX, 128), lambda q: (q, VOX // AUX, 2)),
            pl.BlockSpec((1, STATE), lambda q: (0, 0)),
        ],
        out_specs=pl.BlockSpec((GROUP * 8, CHUNK + TAIL, 128), lambda q: (q, 0, 0)),
        out_shape=jax.ShapeDtypeStruct((PARTS * 8, CHUNK + TAIL, 128), BF),
        name="last",
        compiler_params=SMALL,
        cost_estimate=STEP_COST,
    )(rate, own, halo, w, noise, current, *table, slab, readout)


def analyse_body(data, var, out):
    extra = data[:, CHUNK : CHUNK + TAIL, :].astype(F32)
    both = jnp.sum(extra, axis=1)
    image, innov = both[:, 0:OBS], both[:, OBS : 2 * OBS]
    anomaly = image - jnp.mean(image, axis=0, keepdims=True)
    flipped = jnp.transpose(anomaly)
    covar = jnp.dot(flipped, anomaly, precision=HIGH, preferred_element_type=F32) / (MEMBERS - 1)
    square = (OBS, OBS)
    covar = covar + jnp.where(iota(square, 0) == iota(square, 1), var[...], 0.0)
    work = jnp.concatenate([covar, flipped], axis=1)
    row = iota((OBS, 2 * OBS), 0)
    for k in range(OBS):
        pivot = work[k : k + 1, :] / work[k : k + 1, k : k + 1]
        work = jnp.where(row == k, pivot, work - work[:, k : k + 1] * pivot)
    solved = work[:, OBS : 2 * OBS]
    mixing = jnp.dot(innov, solved, precision=HIGH, preferred_element_type=F32) / (MEMBERS - 1)
    mixing = mixing - jnp.mean(mixing, axis=1, keepdims=True)
    wide = MEMBERS * 16
    repeat = jnp.where(
        lax.shift_right_logical(iota((wide, MEMBERS), 0), 4) == iota((wide, MEMBERS), 1), 1.0, 0.0
    ).astype(BF)
    tall = dot(repeat, mixing.astype(BF)).astype(BF)
    large = lax.dot_general(tall, repeat, (((1,), (1,)), ((), ())), preferred_element_type=F32)
    same = (iota((wide, wide), 0) & 15) == (iota((wide, wide), 1) & 15)
    large = jnp.where(same, large, 0.0).astype(BF)
    for b in range(CHUNK // 16):
        rows = data[:, b * 16 : (b + 1) * 16, :].reshape(wide, 128)
        result = (rows.astype(F32) + dot(large, rows)).astype(BF).reshape(MEMBERS, 16, 128)
        for m in range(MEMBERS):
            out[m % 8, m // 8, b * 16 : (b + 1) * 16, :] = result[m]


def analyse(data, var):
    return pl.pallas_call(
        analyse_body,
        out_shape=jax.ShapeDtypeStruct((8, 8, CHUNK, 128), BF),
        name="analyse",
        compiler_params=pltpu.CompilerParams(vmem_limit_bytes=32 * 2**20),
    )(data, var)


def finish_body(data, out):
    for j in range(4):
        for c in range(8):
            high, quarter = divmod(c, 4)
            out[j, high * CHUNK : (high + 1) * CHUNK, quarter * 128 : (quarter + 1) * 128] = data[
                c, j
            ].astype(F32)


def finish(data):
    return pl.pallas_call(
        finish_body,
        grid=(2,),
        in_specs=[pl.BlockSpec((8, 4, CHUNK, 128), lambda j: (0, j, 0, 0))],
        out_specs=pl.BlockSpec((4, VOX, STATE), lambda j: (j, 0, 0)),
        out_shape=jax.ShapeDtypeStruct((8, VOX, STATE), F32),
        name="finish",
        compiler_params=SMALL,
    )(data)


def swap(value, axes):
    return lax.all_to_all(value, axes, split_axis=0, concat_axis=0, tiled=True)


def per_device(
    state,
    noise,
    w_local,
    conn_weight,
    conn_index,
    boundary,
    send_pos,
    readout,
    observed,
    obs_value,
    obs_var,
    obs_pert,
):
    here = lax.axis_index("zh")
    group = ("zl", "y")
    slab = prep(
        state, conn_weight, conn_index, boundary, observed, obs_value, obs_var, obs_pert
    )
    slab = swap(slab, group)
    first, *packed = pack(state, noise, boundary)
    edge_rate = slab[:, VOX + AUX :, :].reshape(ROWS, STATE)
    sends = lax.dynamic_slice_in_dim(send_pos, here * PARTS, PARTS, 1)
    source = jnp.arange(RING * PARTS, dtype=jnp.int32)
    base = jnp.remainder(here - source // PARTS, RING) * ROWS + (source % PARTS) * BND
    colmap = jnp.transpose(base[:, None, None] + sends, (1, 0, 2)).reshape(PARTS, 1, HALO)
    own, halo, pick, ahead, begin = tables(slab, colmap)
    first = swap(first, group)
    kicks = {0: (first, None)}
    for steps, array in zip(BATCHES, packed):
        array = swap(array, group)
        for place, t in enumerate(steps):
            kicks[t] = (array, place)
    edge_current = current = None
    rate = slab
    for t in range(STEPS):
        table = [edge_rate]
        for o in range(1, RING):
            table.append(lax.ppermute(edge_rate, "zh", [(i, (i + o) % RING) for i in range(RING)]))
        kick, place = kicks[t]
        if t < STEPS - 1:
            edge_rate, edge_current = edge(t, begin, ahead, w_local, first, table, edge_current)
            current, rate, begin = step(
                rate, own, halo, pick, w_local, kick, place, current, table
            )
        else:
            chunks = last(
                rate, own, halo, w_local, kick, place, current, table, slab, readout[None, :]
            )
    gathered = swap(chunks, ("zl", "y", "x", "core"))
    result = swap(analyse(gathered, obs_var), ("x", "core"))
    return finish(result)


def solution(mesh):
    fine = Mesh(mesh.devices.reshape(RING, 2, 4, 4, 2), ("zh", "zl", "y", "x", "core"))
    dom, member = ("zh", "zl", "y"), ("x", "core")
    in_specs = (
        P(member, dom, None),
        P(None, member, dom, None),
        P(),
        P(None, dom),
        P(None, dom),
        P(dom, None),
        P(),
        P(),
        P(dom, None),
        P(dom, None),
        P(dom, None),
        P(member, dom, None),
    )
    return jax.shard_map(
        per_device, mesh=fine, in_specs=in_specs, out_specs=P(member, dom, None), check_vma=False
    )
```

time: 414 us -> 287 us (0.69)
  blocking collectives: 253 us -> 138 us
  matrix products: 59.6 us -> 0 us
  starting transfers between devices: 12.3 us -> 53.5 us
  Pallas kernels: 0 us -> 36.5 us
  other arithmetic: 23.1 us -> 0.15 us
  between operations: 13.8 us -> 0.33 us
  waiting for transfers between devices: 25.5 us -> 36.8 us
  local copies, waits for them, and re-layouts: 25.9 us -> 20.3 us
    all_to_all x7 -> x6, blocking collectives: 222 us -> 138 us  [swap(): return lax.all_to_all(value, axes, split_axis=0, concat_axis=0, tiled=True)]
    dot_general x20 -> x0, matrix products: 59.3 us -> none  [the longest x8 34.2 us: per_device(): jnp.dot(inputs.reshape(-1, width), w_local, preferred_element_type=jnp.fl...]
    ppermute x0 -> x24, starting transfers between devices: none -> 43.4 us  [per_device(): lax.ppermute(edge_rate, 'zh', [(i, (i + o) % RING) for i in range(RING)])]
    pallas_call x0 -> x20, Pallas kernels: none -> 36.5 us  [the longest x7 13.3 us: step(): pl.pallas_call(functools.partial(step_body, current is not None), grid=(P...]
    all_gather x2 -> x0, blocking collectives: 30.6 us -> none  [the longest x1 17.5 us: per_device(): lax.all_gather(image_local, 'member', axis=0, tiled=True)]
    ppermute x0 -> x24, waiting for transfers between devices: none -> 26 us  [per_device(): lax.ppermute(edge_rate, 'zh', [(i, (i + o) % RING) for i in range(RING)])]
    unnamed x19 -> x84, local copies, waits for them, and re-layouts: 2.36 us -> 19.4 us
    all_to_all x1 -> x2, waiting for transfers between devices: 25.5 us -> 10.7 us  [swap(): return lax.all_to_all(value, axes, split_axis=0, concat_axis=0, tiled=True)]
  transfers between devices with their start and end apart: 2 -> 26, of which waited for: 1 -> 14; matrix products, arithmetic and copies ran while one was open for 6% -> 0% of each run, Pallas kernels for 0% -> 7%
where the time goes in v1:
time: 287 us; the launch traced here: 286 us
  blocking collectives  138 us (48%)
  starting transfers between devices  53.5 us (19%)
  waiting for transfers between devices  36.8 us (13%)
  Pallas kernels  36.5 us (13%)
  local copies, waits for them, and re-layouts  20.3 us (7%)
    all_to_all x6, blocking collectives, swap(): return lax.all_to_all(value, axes, split_axis=0, concat_axis=0, tiled=True)  138 us
    ppermute x24, starting transfers between devices, per_device(): lax.ppermute(edge_rate, 'zh', [(i, (i + o) % RING) for i in range(RING)])  43.4 us
    ppermute x24, waiting for transfers between devices, per_device(): lax.ppermute(edge_rate, 'zh', [(i, (i + o) % RING) for i in range(RING)])  26 us
    unnamed x84, local copies, waits for them, and re-layouts  19.4 us
    pallas_call x7, Pallas kernels, step(): pl.pallas_call(functools.partial(step_body, current is not None), grid=(P...  13.3 us
    all_to_all x2, waiting for transfers between devices, swap(): return lax.all_to_all(value, axes, split_axis=0, concat_axis=0, tiled=True)  10.7 us
    all_to_all x2, starting transfers between devices, swap(): return lax.all_to_all(value, axes, split_axis=0, concat_axis=0, tiled=True)  10.1 us
    pallas_call x1, Pallas kernels, analyse(): pl.pallas_call(analyse_body, out_shape=jax.ShapeDtypeStruct((8, 8, CHUNK,...  8.52 us
  transfers between devices with their start and end apart: 26, of which 14 were waited for; matrix products, arithmetic and copies ran while one was open for 0% of the time, Pallas kernels for 7%

profile of v1, /device:TPU:1, one launch (start us, length us, event | category | flops | bytes accessed | tf_op | source)
XLA Modules:
  0.0 286.0 jit_solution(6375192963564403632)
XLA Ops:
  0.0 2.8 copy-done.1
  4.9 2.7 pack.1
  13.0 6.4 %all-to-all-start.2 = ((bf16[8,1,96,512]{3,2,1,0:T(8,128)(2,1)}), bf16[8,1,96,512]{3,2,1,0:T(8,128)(2,1)}, u32[]{:S(2)}, u32[]{:S(2)}) async-start(bf16[8,1,96,512]{3,2,1,0:T(8,128)(2,1)} %copy-done.16), calls=%async_computation.2 | async-start | bytes 1572864 | tf_op jit(solution)/shard_map/all_to_all | solution.py:396
  20.3 10.7 %all-to-all-done.2.refs_5_ = bf16[8,1,96,512]{3,2,1,0:T(8,128)(2,1)} async-done(((bf16[8,1,96,512]{3,2,1,0:T(8,128)(2,1)}), bf16[8,1,96,512]{3,2,1,0:T(8,128)(2,1)}, u32[]{:S(2)}, u32[]{:S(2)}) %all-to-all-start.2) | async-done | bytes 786464 | tf_op jit(solution)/shard_map/all_to_all | solution.py:396
  31.0 18.1 %all_to_all.40.slab.refs_0_.extra = bf16[8,120,512]{2,1,0:T(8,128)(2,1)} all-to-all(bf16[8,120,512]{2,1,0:T(8,128)(2,1)S(1)} %prep.1), channel_id=1, replica_groups=mesh['zh'=4,'zl'=2,'y'=4,'x'=4,'core'=2] {'zl','y'}, dimensions={0} | all-to-all | bytes 1966080 | tf_op jit(solution)/shard_map/all_to_all | solution.py:396
  49.2 18.8 %all_to_all.41.refs_5_.noise = bf16[8,160,512]{2,1,0:T(8,128)(2,1)S(1)} all-to-all(bf16[8,160,512]{2,1,0:T(8,128)(2,1)S(1)} %copy-done.12), channel_id=1, replica_groups=mesh['zh'=4,'zl'=2,'y'=4,'x'=4,'core'=2] {'zl','y'}, dimensions={0} | all-to-all | bytes 2621440 | tf_op jit(solution)/shard_map/all_to_all | solution.py:396
  67.9 22.3 %all_to_all.42.refs_5_ = bf16[8,2,96,512]{3,2,1,0:T(8,128)(2,1)} all-to-all(bf16[8,2,96,512]{3,2,1,0:T(8,128)(2,1)S(1)} %copy-done.10), channel_id=1, replica_groups=mesh['zh'=4,'zl'=2,'y'=4,'x'=4,'core'=2] {'zl','y'}, dimensions={0} | all-to-all | bytes 3145728 | tf_op jit(solution)/shard_map/all_to_all | solution.py:396
  90.2 19.9 %all_to_all.43.refs_5_ = bf16[8,2,96,512]{3,2,1,0:T(8,128)(2,1)} all-to-all(bf16[8,2,96,512]{3,2,1,0:T(8,128)(2,1)S(1)} %copy-done.8), channel_id=1, replica_groups=mesh['zh'=4,'zl'=2,'y'=4,'x'=4,'core'=2] {'zl','y'}, dimensions={0} | all-to-all | bytes 3145728 | tf_op jit(solution)/shard_map/all_to_all | solution.py:396
  110.1 3.7 %all-to-all-start.5 = ((bf16[8,2,96,512]{3,2,1,0:T(8,128)(2,1)}), bf16[8,2,96,512]{3,2,1,0:T(8,128)(2,1)S(1)}, u32[]{:S(2)}, u32[]{:S(2)}) async-start(bf16[8,2,96,512]{3,2,1,0:T(8,128)(2,1)} %copy-done.4), calls=%async_computation.5 | async-start | bytes 3145728 | tf_op jit(solution)/shard_map/all_to_all | solution.py:396
  114.9 5.1 %collective-permute-start.2 = (bf16[64,512]{1,0:T(8,128)(2,1)S(1)}, bf16[64,512]{1,0:T(8,128)(2,1)S(1)}, u32[]{:S(2)}, u32[]{:S(2)}) collective-permute-start(bf16[64,512]{1,0:T(8,128)(2,1)S(1)} %slice_bitcast_fusion.refs_6_.r0), channel_id=1, source_target_pairs={{0,192},{64,0},{128,64},{192,128},{1,193},{65,1},{129,65},{193,129... | collective-permute-start | bytes 196616 | tf_op jit(solution)/shard_map/ppermute | solution.py:437
  124.5 4.1 %tables.1 = (bf16[8,96,96]{2,1,0:T(8,128)(2,1)S(1)}, bf16[8,96,256]{2,1,0:T(8,128)(2,1)S(1)}, bf16[8,16,96]{2,1,0:T(8,128)(2,1)S(1)}, bf16[64,256]{1,0:T(8,128)(2,1)S(1)}, f32[64,512]{1,0:T(8,128)S(1)}) custom-call(bf16[8,120,512]{2,1,0:T(8,128)(2,1)S(1)} %copy-done.13, s32[8,1,128]{2,1,0:T(1,128)S(1)} %copy.14.colmap), custom_call_target="tpu_custom_call" | custom-call | flops 1000000000 | bytes 10000000 | tf_op jit(solution)/shard_map/tables/pallas_call | solution.py:162
  128.6 6.5 %collective-permute-done.1.refs_8_.r2 = bf16[64,512]{1,0:T(8,128)(2,1)S(1)} collective-permute-done((bf16[64,512]{1,0:T(8,128)(2,1)S(1)}, bf16[64,512]{1,0:T(8,128)(2,1)S(1)}, u32[]{:S(2)}, u32[]{:S(2)}) %collective-permute-start.1) | collective-permute-done | bytes 65568 | tf_op jit(solution)/shard_map/ppermute | solution.py:437
  137.5 2.9 %collective-permute-start.4 = (bf16[64,512]{1,0:T(8,128)(2,1)S(1)}, bf16[64,512]{1,0:T(8,128)(2,1)S(1)}, u32[]{:S(2)}, u32[]{:S(2)}) collective-permute-start(bf16[64,512]{1,0:T(8,128)(2,1)S(1)} %get-tuple-element.57.refs_7_.r0), channel_id=1, source_target_pairs={{0,128},{64,192},{128,0},{192,64},{1,129},{65,193},{129,1},{193,65... | collective-permute-start | bytes 196616 | tf_op jit(solution)/shard_map/ppermute | solution.py:437
  147.2 3.8 %collective-permute-start.7 = (bf16[64,512]{1,0:T(8,128)(2,1)S(1)}, bf16[64,512]{1,0:T(8,128)(2,1)S(1)}, u32[]{:S(2)}, u32[]{:S(2)}) collective-permute-start(bf16[64,512]{1,0:T(8,128)(2,1)S(1)} %get-tuple-element.63.refs_7_.r0), channel_id=1, source_target_pairs={{0,128},{64,192},{128,0},{192,64},{1,129},{65,193},{129,1},{193,65... | collective-permute-start | bytes 196616 | tf_op jit(solution)/shard_map/ppermute | solution.py:437
  151.0 2.6 step.8
  157.7 3.7 %collective-permute-start.10 = (bf16[64,512]{1,0:T(8,128)(2,1)S(1)}, bf16[64,512]{1,0:T(8,128)(2,1)S(1)}, u32[]{:S(2)}, u32[]{:S(2)}) collective-permute-start(bf16[64,512]{1,0:T(8,128)(2,1)S(1)} %get-tuple-element.68.refs_7_.r0), channel_id=1, source_target_pairs={{0,128},{64,192},{128,0},{192,64},{1,129},{65,193},{129,1},{193,65... | collective-permute-start | bytes 196616 | tf_op jit(solution)/shard_map/ppermute | solution.py:437
  165.2 2.5 collective-permute-done.9.refs_8_.r1
  168.9 3.1 %collective-permute-start.13 = (bf16[64,512]{1,0:T(8,128)(2,1)S(1)}, bf16[64,512]{1,0:T(8,128)(2,1)S(1)}, u32[]{:S(2)}, u32[]{:S(2)}) collective-permute-start(bf16[64,512]{1,0:T(8,128)(2,1)S(1)} %get-tuple-element.74.refs_7_.r0), channel_id=1, source_target_pairs={{0,128},{64,192},{128,0},{192,64},{1,129},{65,193},{129,1},{193,65... | collective-permute-start | bytes 196616 | tf_op jit(solution)/shard_map/ppermute | solution.py:437
  189.4 3.2 %collective-permute-start.19 = (bf16[64,512]{1,0:T(8,128)(2,1)S(1)}, bf16[64,512]{1,0:T(8,128)(2,1)S(1)}, u32[]{:S(2)}, u32[]{:S(2)}) collective-permute-start(bf16[64,512]{1,0:T(8,128)(2,1)S(1)} %get-tuple-element.85.refs_7_.r0), channel_id=1, source_target_pairs={{0,128},{64,192},{128,0},{192,64},{1,129},{65,193},{129,1},{193,65... | collective-permute-start | bytes 196616 | tf_op jit(solution)/shard_map/ppermute | solution.py:437
  198.9 2.5 collective-permute-start.23
  214.2 2.7 last.1
  216.9 43.6 %all_to_all.44.data = bf16[64,56,128]{2,1,0:T(8,128)(2,1)S(1)} all-to-all(bf16[64,56,128]{2,1,0:T(8,128)(2,1)S(1)} %last.1), channel_id=1, replica_groups=mesh['zh'=4,'zl'=2,'y'=4,'x'=4,'core'=2] {'zl','y','x','core'}, dimensions={0} | all-to-all | bytes 1835008 | tf_op jit(solution)/shard_map/all_to_all | solution.py:396
  260.6 8.5 %analyse.1 = bf16[8,8,48,128]{3,2,1,0:T(8,128)(2,1)S(1)} custom-call(bf16[64,56,128]{2,1,0:T(8,128)(2,1)S(1)} %all_to_all.44.data, f32[1,64]{1,0:T(1,128)S(1)} %copy-done.26), custom_call_target="tpu_custom_call" | custom-call | tf_op jit(solution)/shard_map/analyse/pallas_call | solution.py:366
  269.1 15.6 %all_to_all.45.data = bf16[8,8,48,128]{3,2,1,0:T(8,128)(2,1)S(1)} all-to-all(bf16[8,8,48,128]{3,2,1,0:T(8,128)(2,1)S(1)} %analyse.1), channel_id=1, replica_groups=mesh['zh'=4,'zl'=2,'y'=4,'x'=4,'core'=2] {'x','core'}, dimensions={0} | all-to-all | bytes 1572864 | tf_op jit(solution)/shard_map/all_to_all | solution.py:396
  (142 shorter events, 69.6 us)
Async XLA Ops:
  13.0 18.0 %all-to-all-start.2 = ((bf16[8,1,96,512]{3,2,1,0:T(8,128)(2,1)}), bf16[8,1,96,512]{3,2,1,0:T(8,128)(2,1)}, u32[]{:S(2)}, u32[]{:S(2)}) async-start(bf16[8,1,96,512]{3,2,1,0:T(8,128)(2,1)} %copy-done.16), calls=%async_computation.2 | async-start | bytes 1572864 | tf_op jit(solution)/shard_map/all_to_all | solution.py:396
  110.1 94.7 %all-to-all-start.5 = ((bf16[8,2,96,512]{3,2,1,0:T(8,128)(2,1)}), bf16[8,2,96,512]{3,2,1,0:T(8,128)(2,1)S(1)}, u32[]{:S(2)}, u32[]{:S(2)}) async-start(bf16[8,2,96,512]{3,2,1,0:T(8,128)(2,1)} %copy-done.4), calls=%async_computation.5 | async-start | bytes 3145728 | tf_op jit(solution)/shard_map/all_to_all | solution.py:396
  114.9 13.7 %collective-permute-start.2 = (bf16[64,512]{1,0:T(8,128)(2,1)S(1)}, bf16[64,512]{1,0:T(8,128)(2,1)S(1)}, u32[]{:S(2)}, u32[]{:S(2)}) collective-permute-start(bf16[64,512]{1,0:T(8,128)(2,1)S(1)} %slice_bitcast_fusion.refs_6_.r0), channel_id=1, source_target_pairs={{0,192},{64,0},{128,64},{192,128},{1,193},{65,1},{129,65},{193,129... | collective-permute-start | bytes 196616 | tf_op jit(solution)/shard_map/ppermute | solution.py:437
  120.1 15.1 %collective-permute-start.1 = (bf16[64,512]{1,0:T(8,128)(2,1)S(1)}, bf16[64,512]{1,0:T(8,128)(2,1)S(1)}, u32[]{:S(2)}, u32[]{:S(2)}) collective-permute-start(bf16[64,512]{1,0:T(8,128)(2,1)S(1)} %slice_bitcast_fusion.refs_6_.r0), channel_id=1, source_target_pairs={{0,128},{64,192},{128,0},{192,64},{1,129},{65,193},{129,1},{193,65... | collective-permute-start | bytes 196616 | tf_op jit(solution)/shard_map/ppermute | solution.py:437
  121.2 15.4 %collective-permute-start = (bf16[64,512]{1,0:T(8,128)(2,1)S(1)}, bf16[64,512]{1,0:T(8,128)(2,1)S(1)}, u32[]{:S(2)}, u32[]{:S(2)}) collective-permute-start(bf16[64,512]{1,0:T(8,128)(2,1)S(1)} %slice_bitcast_fusion.refs_6_.r0), channel_id=1, source_target_pairs={{0,64},{64,128},{128,192},{192,0},{1,65},{65,129},{129,193},{193,1... | collective-permute-start | bytes 196616 | tf_op jit(solution)/shard_map/ppermute | solution.py:437
  137.5 7.1 %collective-permute-start.4 = (bf16[64,512]{1,0:T(8,128)(2,1)S(1)}, bf16[64,512]{1,0:T(8,128)(2,1)S(1)}, u32[]{:S(2)}, u32[]{:S(2)}) collective-permute-start(bf16[64,512]{1,0:T(8,128)(2,1)S(1)} %get-tuple-element.57.refs_7_.r0), channel_id=1, source_target_pairs={{0,128},{64,192},{128,0},{192,64},{1,129},{65,193},{129,1},{193,65... | collective-permute-start | bytes 196616 | tf_op jit(solution)/shard_map/ppermute | solution.py:437
  140.5 5.3 %collective-permute-start.3 = (bf16[64,512]{1,0:T(8,128)(2,1)S(1)}, bf16[64,512]{1,0:T(8,128)(2,1)S(1)}, u32[]{:S(2)}, u32[]{:S(2)}) collective-permute-start(bf16[64,512]{1,0:T(8,128)(2,1)S(1)} %get-tuple-element.57.refs_7_.r0), channel_id=1, source_target_pairs={{0,64},{64,128},{128,192},{192,0},{1,65},{65,129},{129,193},{193,1... | collective-permute-start | bytes 196616 | tf_op jit(solution)/shard_map/ppermute | solution.py:437
  146.1 7.5 %collective-permute-start.8 = (bf16[64,512]{1,0:T(8,128)(2,1)S(1)}, bf16[64,512]{1,0:T(8,128)(2,1)S(1)}, u32[]{:S(2)}, u32[]{:S(2)}) collective-permute-start(bf16[64,512]{1,0:T(8,128)(2,1)S(1)} %get-tuple-element.63.refs_7_.r0), channel_id=1, source_target_pairs={{0,192},{64,0},{128,64},{192,128},{1,193},{65,1},{129,65},{193,129... | collective-permute-start | bytes 196616 | tf_op jit(solution)/shard_map/ppermute | solution.py:437
  147.2 7.7 %collective-permute-start.7 = (bf16[64,512]{1,0:T(8,128)(2,1)S(1)}, bf16[64,512]{1,0:T(8,128)(2,1)S(1)}, u32[]{:S(2)}, u32[]{:S(2)}) collective-permute-start(bf16[64,512]{1,0:T(8,128)(2,1)S(1)} %get-tuple-element.63.refs_7_.r0), channel_id=1, source_target_pairs={{0,128},{64,192},{128,0},{192,64},{1,129},{65,193},{129,1},{193,65... | collective-permute-start | bytes 196616 | tf_op jit(solution)/shard_map/ppermute | solution.py:437
  151.0 5.4 %collective-permute-start.6 = (bf16[64,512]{1,0:T(8,128)(2,1)S(1)}, bf16[64,512]{1,0:T(8,128)(2,1)S(1)}, u32[]{:S(2)}, u32[]{:S(2)}) collective-permute-start(bf16[64,512]{1,0:T(8,128)(2,1)S(1)} %get-tuple-element.63.refs_7_.r0), channel_id=1, source_target_pairs={{0,64},{64,128},{128,192},{192,0},{1,65},{65,129},{129,193},{193,1... | collective-permute-start | bytes 196616 | tf_op jit(solution)/shard_map/ppermute | solution.py:437
  156.7 6.3 %collective-permute-start.11 = (bf16[64,512]{1,0:T(8,128)(2,1)S(1)}, bf16[64,512]{1,0:T(8,128)(2,1)S(1)}, u32[]{:S(2)}, u32[]{:S(2)}) collective-permute-start(bf16[64,512]{1,0:T(8,128)(2,1)S(1)} %get-tuple-element.68.refs_7_.r0), channel_id=1, source_target_pairs={{0,192},{64,0},{128,64},{192,128},{1,193},{65,1},{129,65},{193,129... | collective-permute-start | bytes 196616 | tf_op jit(solution)/shard_map/ppermute | solution.py:437
  157.7 7.5 %collective-permute-start.10 = (bf16[64,512]{1,0:T(8,128)(2,1)S(1)}, bf16[64,512]{1,0:T(8,128)(2,1)S(1)}, u32[]{:S(2)}, u32[]{:S(2)}) collective-permute-start(bf16[64,512]{1,0:T(8,128)(2,1)S(1)} %get-tuple-element.68.refs_7_.r0), channel_id=1, source_target_pairs={{0,128},{64,192},{128,0},{192,64},{1,129},{65,193},{129,1},{193,65... | collective-permute-start | bytes 196616 | tf_op jit(solution)/shard_map/ppermute | solution.py:437
  161.4 6.3 %collective-permute-start.9 = (bf16[64,512]{1,0:T(8,128)(2,1)S(1)}, bf16[64,512]{1,0:T(8,128)(2,1)S(1)}, u32[]{:S(2)}, u32[]{:S(2)}) collective-permute-start(bf16[64,512]{1,0:T(8,128)(2,1)S(1)} %get-tuple-element.68.refs_7_.r0), channel_id=1, source_target_pairs={{0,64},{64,128},{128,192},{192,0},{1,65},{65,129},{129,193},{193,1... | collective-permute-start | bytes 196616 | tf_op jit(solution)/shard_map/ppermute | solution.py:437
  168.0 6.4 %collective-permute-start.14 = (bf16[64,512]{1,0:T(8,128)(2,1)S(1)}, bf16[64,512]{1,0:T(8,128)(2,1)S(1)}, u32[]{:S(2)}, u32[]{:S(2)}) collective-permute-start(bf16[64,512]{1,0:T(8,128)(2,1)S(1)} %get-tuple-element.74.refs_7_.r0), channel_id=1, source_target_pairs={{0,192},{64,0},{128,64},{192,128},{1,193},{65,1},{129,65},{193,129... | collective-permute-start | bytes 196616 | tf_op jit(solution)/shard_map/ppermute | solution.py:437
  168.9 7.1 %collective-permute-start.13 = (bf16[64,512]{1,0:T(8,128)(2,1)S(1)}, bf16[64,512]{1,0:T(8,128)(2,1)S(1)}, u32[]{:S(2)}, u32[]{:S(2)}) collective-permute-start(bf16[64,512]{1,0:T(8,128)(2,1)S(1)} %get-tuple-element.74.refs_7_.r0), channel_id=1, source_target_pairs={{0,128},{64,192},{128,0},{192,64},{1,129},{65,193},{129,1},{193,65... | collective-permute-start | bytes 196616 | tf_op jit(solution)/shard_map/ppermute | solution.py:437
  172.0 6.3 %collective-permute-start.12 = (bf16[64,512]{1,0:T(8,128)(2,1)S(1)}, bf16[64,512]{1,0:T(8,128)(2,1)S(1)}, u32[]{:S(2)}, u32[]{:S(2)}) collective-permute-start(bf16[64,512]{1,0:T(8,128)(2,1)S(1)} %get-tuple-element.74.refs_7_.r0), channel_id=1, source_target_pairs={{0,64},{64,128},{128,192},{192,0},{1,65},{65,129},{129,193},{193,1... | collective-permute-start | bytes 196616 | tf_op jit(solution)/shard_map/ppermute | solution.py:437
  178.6 6.4 %collective-permute-start.17 = (bf16[64,512]{1,0:T(8,128)(2,1)S(1)}, bf16[64,512]{1,0:T(8,128)(2,1)S(1)}, u32[]{:S(2)}, u32[]{:S(2)}) collective-permute-start(bf16[64,512]{1,0:T(8,128)(2,1)S(1)} %get-tuple-element.79.refs_7_.r0), channel_id=1, source_target_pairs={{0,192},{64,0},{128,64},{192,128},{1,193},{65,1},{129,65},{193,129... | collective-permute-start | bytes 196616 | tf_op jit(solution)/shard_map/ppermute | solution.py:437
  180.2 7.1 %collective-permute-start.16 = (bf16[64,512]{1,0:T(8,128)(2,1)S(1)}, bf16[64,512]{1,0:T(8,128)(2,1)S(1)}, u32[]{:S(2)}, u32[]{:S(2)}) collective-permute-start(bf16[64,512]{1,0:T(8,128)(2,1)S(1)} %get-tuple-element.79.refs_7_.r0), channel_id=1, source_target_pairs={{0,128},{64,192},{128,0},{192,64},{1,129},{65,193},{129,1},{193,65... | collective-permute-start | bytes 196616 | tf_op jit(solution)/shard_map/ppermute | solution.py:437
  182.0 5.9 %collective-permute-start.15 = (bf16[64,512]{1,0:T(8,128)(2,1)S(1)}, bf16[64,512]{1,0:T(8,128)(2,1)S(1)}, u32[]{:S(2)}, u32[]{:S(2)}) collective-permute-start(bf16[64,512]{1,0:T(8,128)(2,1)S(1)} %get-tuple-element.79.refs_7_.r0), channel_id=1, source_target_pairs={{0,64},{64,128},{128,192},{192,0},{1,65},{65,129},{129,193},{193,1... | collective-permute-start | bytes 196616 | tf_op jit(solution)/shard_map/ppermute | solution.py:437
  188.3 9.2 %collective-permute-start.20 = (bf16[64,512]{1,0:T(8,128)(2,1)S(1)}, bf16[64,512]{1,0:T(8,128)(2,1)S(1)}, u32[]{:S(2)}, u32[]{:S(2)}) collective-permute-start(bf16[64,512]{1,0:T(8,128)(2,1)S(1)} %get-tuple-element.85.refs_7_.r0), channel_id=1, source_target_pairs={{0,192},{64,0},{128,64},{192,128},{1,193},{65,1},{129,65},{193,129... | collective-permute-start | bytes 196616 | tf_op jit(solution)/shard_map/ppermute | solution.py:437
  189.4 8.1 %collective-permute-start.19 = (bf16[64,512]{1,0:T(8,128)(2,1)S(1)}, bf16[64,512]{1,0:T(8,128)(2,1)S(1)}, u32[]{:S(2)}, u32[]{:S(2)}) collective-permute-start(bf16[64,512]{1,0:T(8,128)(2,1)S(1)} %get-tuple-element.85.refs_7_.r0), channel_id=1, source_target_pairs={{0,128},{64,192},{128,0},{192,64},{1,129},{65,193},{129,1},{193,65... | collective-permute-start | bytes 196616 | tf_op jit(solution)/shard_map/ppermute | solution.py:437
  198.9 15.2 %collective-permute-start.23 = (bf16[64,512]{1,0:T(8,128)(2,1)}, bf16[64,512]{1,0:T(8,128)(2,1)}, u32[]{:S(2)}, u32[]{:S(2)}) collective-permute-start(bf16[64,512]{1,0:T(8,128)(2,1)} %get-tuple-element.90.r0), channel_id=1, source_target_pairs={{0,192},{64,0},{128,64},{192,128},{1,193},{65,1},{129,65},{193,129... | collective-permute-start | bytes 196616 | tf_op jit(solution)/shard_map/ppermute | solution.py:437
  201.4 12.7 %collective-permute-start.22 = (bf16[64,512]{1,0:T(8,128)(2,1)}, bf16[64,512]{1,0:T(8,128)(2,1)}, u32[]{:S(2)}, u32[]{:S(2)}) collective-permute-start(bf16[64,512]{1,0:T(8,128)(2,1)} %get-tuple-element.90.r0), channel_id=1, source_target_pairs={{0,128},{64,192},{128,0},{192,64},{1,129},{65,193},{129,1},{193,65... | collective-permute-start | bytes 196616 | tf_op jit(solution)/shard_map/ppermute | solution.py:437
  203.3 10.8 %collective-permute-start.21 = (bf16[64,512]{1,0:T(8,128)(2,1)}, bf16[64,512]{1,0:T(8,128)(2,1)}, u32[]{:S(2)}, u32[]{:S(2)}) collective-permute-start(bf16[64,512]{1,0:T(8,128)(2,1)} %get-tuple-element.90.r0), channel_id=1, source_target_pairs={{0,64},{64,128},{128,192},{192,0},{1,65},{65,129},{129,193},{193,1... | collective-permute-start | bytes 196616 | tf_op jit(solution)/shard_map/ppermute | solution.py:437
  (44 other events, 393.0 us)

commit v2 on v1

--- a/solution.py
+++ b/solution.py
@@ -16,6 +16,7 @@
 HALO = 128
 PARTS = 8
 RING = 4
+DEPTH, WIDTH, LENGTH, CORES = 8, 4, 4, 2
 ROWS = PARTS * BND
 AUX = 16
 TAIL = 8
@@ -57,7 +58,7 @@
     return jnp.where(match, 1.0, 0.0).astype(BF)
 
 
-def prep_body(state, weight, index, bound, observed, value, var, pert, slab):
+def prep_body(state, noise, weight, index, bound, observed, value, var, pert, slab):
     chosen = chosen_rows(bound[...])
     for j in range(2):
         rate = jnp.tanh(state[j]).astype(BF)
@@ -69,9 +70,13 @@
         info = (observed[...].astype(F32),) + pieces(shifted)
         slab[j, VOX : VOX + AUX, 256 : 256 + OBS] = stack_rows(info, (AUX, OBS)).astype(BF)
         slab[j, VOX : VOX + AUX, 384:512] = chosen
-        slab[j, VOX + AUX : VOX + AUX + BND, :] = dot(chosen[:, 0:VOX], rate)[0:BND].astype(BF)
-
-
+        start = (0.5 * state[j] + noise[0, j].astype(F32)).astype(BF)
+        pick = chosen[:, 0:VOX]
+        both = (dot(pick, rate)[0:BND], dot(pick, start)[0:BND])
+        slab[j, VOX + AUX : VOX + 2 * AUX, :] = jnp.concatenate(both, axis=0).astype(BF)
+
+
+ROOMY = tuple(range(8))
 SMALL = pltpu.CompilerParams(vmem_limit_bytes=20 * 2**20)
 
 
@@ -79,12 +84,13 @@
     return pl.BlockSpec(shape, lambda q: (0,) * len(shape))
 
 
-def prep(state, weight, index, bound, observed, value, var, pert):
+def prep(state, noise, weight, index, bound, observed, value, var, pert):
     return pl.pallas_call(
         prep_body,
         grid=(PARTS // 2,),
         in_specs=[
             pl.BlockSpec((2, VOX, STATE), lambda j: (j, 0, 0)),
+            pl.BlockSpec((1, 2, VOX, STATE), lambda j: (0, j, 0, 0)),
             whole(KIN, VOX),
             whole(KIN, VOX),
             whole(1, BND),
@@ -93,26 +99,27 @@
             whole(1, OBS),
             pl.BlockSpec((2, 1, OBS), lambda j: (j, 0, 0)),
         ],
-        out_specs=pl.BlockSpec((2, VOX + AUX + BND, STATE), lambda j: (j, 0, 0)),
-        out_shape=jax.ShapeDtypeStruct((PARTS, VOX + AUX + BND, STATE), BF),
+        out_specs=pl.BlockSpec((2, VOX + 2 * AUX, STATE), lambda j: (j, 0, 0)),
+        out_shape=jax.ShapeDtypeStruct((PARTS, VOX + 2 * AUX, STATE), BF),
         name="prep",
-        compiler_params=SMALL,
-    )(state, weight, index, bound, observed, value, var, pert)
+    )(state, noise, weight, index, bound, observed, value, var, pert)
 
 
 def pack_body(state, noise, bound, first, *packed):
     chosen = chosen_rows(bound[...])[:, 0:VOX]
     start = (0.5 * state[0] + noise[0, 0].astype(F32)).astype(BF)
     first[0, 0:VOX, :] = start
-    for t in range(STEPS):
-        rows = start if t == 0 else noise[t, 0]
-        first[0, VOX + t * BND : VOX + (t + 1) * BND, :] = dot(chosen, rows)[0:BND].astype(BF)
+    found = [dot(chosen, noise[t, 0])[0:BND].astype(BF) for t in range(1, STEPS)]
+    found.append(jnp.zeros((BND, STATE), BF))
+    first[0, VOX:, :] = found[0]
     for steps, out in zip(BATCHES, packed):
         for place, t in enumerate(steps):
-            out[0, place] = noise[t, 0]
-
-
-BATCHES = ((1,), (2, 3), (4, 5), (6, 7))
+            out[0, place, 0:VOX, :] = noise[t, 0]
+            out[0, place, VOX:, :] = found[t]
+
+
+BATCHES = ((1,), (2,), (3,), (4, 5), (6, 7))
+FIRST = VOX + BND
 
 
 def pack(state, noise, bound):
@@ -125,12 +132,11 @@
             pl.BlockSpec((STEPS, 1, VOX, STATE), lambda j: (0, j, 0, 0)),
             whole(1, BND),
         ],
-        out_specs=[pl.BlockSpec((1, VOX + STEPS * BND, STATE), lambda j: (j, 0, 0))]
-        + [pl.BlockSpec((1, n, VOX, STATE), lambda j: (j, 0, 0, 0)) for n in sizes],
-        out_shape=[jax.ShapeDtypeStruct((PARTS, VOX + STEPS * BND, STATE), BF)]
-        + [jax.ShapeDtypeStruct((PARTS, n, VOX, STATE), BF) for n in sizes],
+        out_specs=[pl.BlockSpec((1, FIRST, STATE), lambda j: (j, 0, 0))]
+        + [pl.BlockSpec((1, n, FIRST, STATE), lambda j: (j, 0, 0, 0)) for n in sizes],
+        out_shape=[jax.ShapeDtypeStruct((PARTS, FIRST, STATE), BF)]
+        + [jax.ShapeDtypeStruct((PARTS, n, FIRST, STATE), BF) for n in sizes],
         name="pack",
-        compiler_params=SMALL,
         cost_estimate=pl.CostEstimate(flops=10**9, bytes_accessed=14 * 10**6, transcendentals=0),
     )(state, noise, bound)
 
@@ -197,8 +203,13 @@
     rate_out[...] = jnp.tanh(value).astype(BF)
 
 
-def edge(t, begin, ahead, w, first, table, current):
+def edge(begin, ahead, w, noise, place, table, current):
     more = [] if current is None else [current]
+    kind, place = place
+    if kind == "rows":
+        early = pl.BlockSpec((PARTS, BND, STATE), lambda q: (0, place, 0))
+    else:
+        early = pl.BlockSpec((PARTS, 1, BND, STATE), lambda q: (0, place, VOX // BND, 0))
     return pl.pallas_call(
         edge_body,
         grid=(1,),
@@ -206,7 +217,7 @@
             whole(ROWS, STATE),
             whole(ROWS, RING * ROWS),
             whole(STATE, STATE),
-            pl.BlockSpec((PARTS, BND, STATE), lambda q: (0, VOX // BND + t, 0)),
+            early,
         ]
         + [whole(ROWS, STATE)] * (RING + len(more)),
         out_specs=[whole(ROWS, STATE), whole(ROWS, STATE)],
@@ -217,7 +228,7 @@
         name="edge",
         compiler_params=SMALL,
         cost_estimate=pl.CostEstimate(flops=10**8, bytes_accessed=10**6, transcendentals=0),
-    )(begin, ahead, w, first, *table, *more)
+    )(begin, ahead, w, noise, *table, *more)
 
 
 GROUP = 4
@@ -253,8 +264,10 @@
 
 def common_specs(has_current, with_pick, place):
     part = lambda *shape: pl.BlockSpec((GROUP,) + shape, lambda q: (q, 0, 0))
-    kick = part(VOX, STATE)
-    if place is not None:
+    kind, place = place
+    if kind == "rows":
+        kick = pl.BlockSpec((GROUP, VOX, STATE), lambda q: (q, place, 0))
+    else:
         kick = pl.BlockSpec((GROUP, 1, VOX, STATE), lambda q: (q, place, 0, 0))
     specs = [part(VOX, STATE), part(VOX, VOX), part(VOX, RING * ROWS)]
     if with_pick:
@@ -269,7 +282,7 @@
 STEP_COST = pl.CostEstimate(flops=2 * 10**9, bytes_accessed=6 * 10**6, transcendentals=4 * 10**5)
 
 
-def step(rate, own, halo, pick, w, noise, place, current, table):
+def step(roomy, rate, own, halo, pick, w, noise, place, current, table):
     args = [rate, own, halo, pick, w, noise] + ([] if current is None else [current]) + list(table)
     return pl.pallas_call(
         functools.partial(step_body, current is not None),
@@ -286,7 +299,7 @@
             jax.ShapeDtypeStruct((ROWS, STATE), F32),
         ],
         name="step",
-        compiler_params=SMALL,
+        compiler_params=None if roomy else SMALL,
         cost_estimate=STEP_COST,
     )(*args)
 
@@ -330,7 +343,11 @@
     )(rate, own, halo, w, noise, current, *table, slab, readout)
 
 
-def analyse_body(data, var, out):
+def analyse_body(core, kept, other, var, out, data):
+    half = MEMBERS // 2
+    is_first = core[0] == 0
+    data[0:half] = jnp.where(is_first, kept[...], other[...])
+    data[half:] = jnp.where(is_first, other[...], kept[...])
     extra = data[:, CHUNK : CHUNK + TAIL, :].astype(F32)
     both = jnp.sum(extra, axis=1)
     image, innov = both[:, 0:OBS], both[:, OBS : 2 * OBS]
@@ -341,9 +358,15 @@
     covar = covar + jnp.where(iota(square, 0) == iota(square, 1), var[...], 0.0)
     work = jnp.concatenate([covar, flipped], axis=1)
     row = iota((OBS, 2 * OBS), 0)
-    for k in range(OBS):
-        pivot = work[k : k + 1, :] / work[k : k + 1, k : k + 1]
-        work = jnp.where(row == k, pivot, work - work[:, k : k + 1] * pivot)
+    for k in range(0, OBS, 2):
+        upper, lower = work[k : k + 1, :], work[k + 1 : k + 2, :]
+        a, b = upper[:, k : k + 1], upper[:, k + 1 : k + 2]
+        c, d = lower[:, k : k + 1], lower[:, k + 1 : k + 2]
+        scale = 1.0 / (a * d - b * c)
+        one = (d * upper - b * lower) * scale
+        two = (a * lower - c * upper) * scale
+        rest = work - work[:, k : k + 1] * one - work[:, k + 1 : k + 2] * two
+        work = jnp.where(row == k, one, jnp.where(row == k + 1, two, rest))
     solved = work[:, OBS : 2 * OBS]
     mixing = jnp.dot(innov, solved, precision=HIGH, preferred_element_type=F32) / (MEMBERS - 1)
     mixing = mixing - jnp.mean(mixing, axis=1, keepdims=True)
@@ -359,16 +382,21 @@
         rows = data[:, b * 16 : (b + 1) * 16, :].reshape(wide, 128)
         result = (rows.astype(F32) + dot(large, rows)).astype(BF).reshape(MEMBERS, 16, 128)
         for m in range(MEMBERS):
-            out[m % 8, m // 8, b * 16 : (b + 1) * 16, :] = result[m]
-
-
-def analyse(data, var):
+            owner = (m % LENGTH) * CORES + m // half
+            out[owner, m % half // LENGTH, b * 16 : (b + 1) * 16, :] = result[m]
+
+
+def analyse(core, kept, other, var):
+    vmem = pl.BlockSpec(memory_space=pltpu.VMEM)
     return pl.pallas_call(
         analyse_body,
+        in_specs=[pl.BlockSpec(memory_space=pltpu.SMEM), vmem, vmem, vmem],
+        out_specs=vmem,
+        scratch_shapes=[pltpu.VMEM((MEMBERS, CHUNK + TAIL, 128), BF)],
         out_shape=jax.ShapeDtypeStruct((8, 8, CHUNK, 128), BF),
         name="analyse",
         compiler_params=pltpu.CompilerParams(vmem_limit_bytes=32 * 2**20),
-    )(data, var)
+    )(core, kept, other, var)
 
 
 def finish_body(data, out):
@@ -392,8 +420,39 @@
     )(data)
 
 
-def swap(value, axes):
-    return lax.all_to_all(value, axes, split_axis=0, concat_axis=0, tiled=True)
+def pair(ring, low, core):
+    return (2 * ring + low + core) % DEPTH
+
+
+GROUPS = [
+    [
+        (pair(ring, low, core) * WIDTH + y) * CORES + core
+        for low in range(2)
+        for y in range(WIDTH)
+    ]
+    for core in range(CORES)
+    for ring in range(RING)
+]
+WIDE_GROUPS = [
+    [
+        ((pair(ring, low, core) * WIDTH + y) * LENGTH + x) * CORES + core
+        for low in range(2)
+        for y in range(WIDTH)
+        for x in range(LENGTH)
+    ]
+    for core in range(CORES)
+    for ring in range(RING)
+]
+
+
+def swap(value, axes, groups=None):
+    return lax.all_to_all(
+        value, axes, split_axis=0, concat_axis=0, tiled=True, axis_index_groups=groups
+    )
+
+
+def trade(value):
+    return swap(value, ("z", "y", "core"), GROUPS)
 
 
 def per_device(
@@ -410,49 +469,71 @@
     obs_var,
     obs_pert,
 ):
-    here = lax.axis_index("zh")
-    group = ("zl", "y")
+    core = lax.axis_index("core")
+    here = jnp.remainder(lax.axis_index("z") - core, DEPTH) // 2
     slab = prep(
-        state, conn_weight, conn_index, boundary, observed, obs_value, obs_var, obs_pert
+        state, noise, conn_weight, conn_index, boundary, observed, obs_value, obs_var, obs_pert
     )
-    slab = swap(slab, group)
+    slab = trade(slab)
     first, *packed = pack(state, noise, boundary)
-    edge_rate = slab[:, VOX + AUX :, :].reshape(ROWS, STATE)
-    sends = lax.dynamic_slice_in_dim(send_pos, here * PARTS, PARTS, 1)
+    edge_rate = slab[:, VOX + AUX : VOX + AUX + BND, :].reshape(ROWS, STATE)
+    sends = jnp.concatenate(
+        [
+            lax.dynamic_slice_in_dim(send_pos, pair(here, low, core) * WIDTH, WIDTH, 1)
+            for low in range(2)
+        ],
+        axis=1,
+    )
     source = jnp.arange(RING * PARTS, dtype=jnp.int32)
-    base = jnp.remainder(here - source // PARTS, RING) * ROWS + (source % PARTS) * BND
+    level = jnp.remainder(source // WIDTH - core, DEPTH)
+    base = jnp.remainder(here - level // 2, RING) * ROWS
+    base = base + ((level % 2) * WIDTH + source % WIDTH) * BND
     colmap = jnp.transpose(base[:, None, None] + sends, (1, 0, 2)).reshape(PARTS, 1, HALO)
     own, halo, pick, ahead, begin = tables(slab, colmap)
-    first = swap(first, group)
-    kicks = {0: (first, None)}
+    first = trade(first)
+    kicks = {0: (first, ("rows", 0))}
     for steps, array in zip(BATCHES, packed):
-        array = swap(array, group)
+        array = trade(array)
         for place, t in enumerate(steps):
-            kicks[t] = (array, place)
+            kicks[t] = (array, ("batch", place))
     edge_current = current = None
     rate = slab
     for t in range(STEPS):
         table = [edge_rate]
         for o in range(1, RING):
-            table.append(lax.ppermute(edge_rate, "zh", [(i, (i + o) % RING) for i in range(RING)]))
+            table.append(
+                lax.ppermute(edge_rate, "z", [(i, (i + 2 * o) % DEPTH) for i in range(DEPTH)])
+            )
         kick, place = kicks[t]
         if t < STEPS - 1:
-            edge_rate, edge_current = edge(t, begin, ahead, w_local, first, table, edge_current)
+            if t == 0:
+                found, row = slab, ("rows", (VOX + AUX) // BND + 1)
+            elif t == 1:
+                found, row = first, ("rows", VOX // BND)
+            else:
+                found, row = kicks[t - 1]
+            edge_rate, edge_current = edge(begin, ahead, w_local, found, row, table, edge_current)
             current, rate, begin = step(
-                rate, own, halo, pick, w_local, kick, place, current, table
+                t in ROOMY, rate, own, halo, pick, w_local, kick, place, current, table
             )
         else:
             chunks = last(
                 rate, own, halo, w_local, kick, place, current, table, slab, readout[None, :]
             )
-    gathered = swap(chunks, ("zl", "y", "x", "core"))
-    result = swap(analyse(gathered, obs_var), ("x", "core"))
+    wide = chunks.reshape(PARTS * LENGTH, CORES, CHUNK + TAIL, 128)
+    wide = swap(wide, ("z", "y", "x", "core"), WIDE_GROUPS)
+    kept = lax.dynamic_index_in_dim(wide, core, 1, keepdims=False)
+    other = lax.dynamic_index_in_dim(wide, 1 - core, 1, keepdims=False)
+    other = lax.ppermute(other, "core", [(0, 1), (1, 0)])
+    result = swap(analyse(core.reshape(1), kept, other, obs_var), ("x", "core"))
     return finish(result)
 
 
 def solution(mesh):
-    fine = Mesh(mesh.devices.reshape(RING, 2, 4, 4, 2), ("zh", "zl", "y", "x", "core"))
-    dom, member = ("zh", "zl", "y"), ("x", "core")
+    fine = Mesh(
+        mesh.devices.reshape(DEPTH, WIDTH, LENGTH, CORES), ("z", "y", "x", "core")
+    )
+    dom, member = ("z", "y"), ("x", "core")
     in_specs = (
         P(member, dom, None),
         P(None, member, dom, None),

time: 287 us -> 306 us (1.066)
  Pallas kernels: 36.5 us -> 66 us
  starting transfers between devices: 53.5 us -> 81.7 us
  blocking collectives: 138 us -> 116 us
  local copies, waits for them, and re-layouts: 20.3 us -> 10.2 us
  waiting for transfers between devices: 36.8 us -> 30.6 us
    all_to_all x6, blocking collectives: 138 us -> 116 us  [swap(): lax.all_to_all(value, axes, split_axis=0, concat_axis=0, tiled=True, axis...]
    ppermute x24 -> x25, starting transfers between devices: 43.4 us -> 64.5 us  [the longest x24 49.6 us: per_device(): lax.ppermute(edge_rate, 'z', [(i, (i + 2 * o) % DEPTH) for i in range(DEP...]
    pallas_call x7, Pallas kernels: 13.3 us -> 30.7 us  [step(): pl.pallas_call(functools.partial(step_body, current is not None), grid=(P...]
    ppermute x24 -> x25, waiting for transfers between devices: 26 us -> 12.2 us  [the longest x24 10.8 us: per_device(): lax.ppermute(edge_rate, 'z', [(i, (i + 2 * o) % DEPTH) for i in range(DEP...]
    unnamed x84 -> x130, local copies, waits for them, and re-layouts: 19.4 us -> 9.85 us
    all_to_all x2 -> x3, waiting for transfers between devices: 10.7 us -> 18.4 us  [swap(): lax.all_to_all(value, axes, split_axis=0, concat_axis=0, tiled=True, axis...]
    all_to_all x2 -> x3, starting transfers between devices: 10.1 us -> 17.2 us  [swap(): lax.all_to_all(value, axes, split_axis=0, concat_axis=0, tiled=True, axis...]
    pallas_call x1, Pallas kernels: 2.71 us -> 8.83 us  [pack(): pl.pallas_call(pack_body, grid=(PARTS,), in_specs=[pl.BlockSpec((1, VOX,...]
  transfers between devices with their start and end apart: 26 -> 28, of which waited for: 14 -> 10; matrix products, arithmetic and copies ran while one was open for 0% -> 0% of each run, Pallas kernels for 7% -> 14%
where the time goes in v2:
time: 306 us; the launch traced here: 305 us
  blocking collectives  116 us (38%)
  starting transfers between devices  81.7 us (27%)
  Pallas kernels  66 us (22%)
  waiting for transfers between devices  30.6 us (10%)
  local copies, waits for them, and re-layouts  10.2 us (3%)
    all_to_all x6, blocking collectives, swap(): lax.all_to_all(value, axes, split_axis=0, concat_axis=0, tiled=True, axis...  116 us
    ppermute x24, starting transfers between devices, per_device(): lax.ppermute(edge_rate, 'z', [(i, (i + 2 * o) % DEPTH) for i in range(DEP...  49.6 us
    pallas_call x7, Pallas kernels, step(): pl.pallas_call(functools.partial(step_body, current is not None), grid=(P...  30.7 us
    all_to_all x3, waiting for transfers between devices, swap(): lax.all_to_all(value, axes, split_axis=0, concat_axis=0, tiled=True, axis...  18.4 us
    all_to_all x3, starting transfers between devices, swap(): lax.all_to_all(value, axes, split_axis=0, concat_axis=0, tiled=True, axis...  17.2 us
    ppermute x1, starting transfers between devices, per_device(): other = lax.ppermute(other, 'core', [(0, 1), (1, 0)])  14.9 us
    ppermute x24, waiting for transfers between devices, per_device(): lax.ppermute(edge_rate, 'z', [(i, (i + 2 * o) % DEPTH) for i in range(DEP...  10.8 us
    pallas_call x1, Pallas kernels, analyse(): pl.pallas_call(analyse_body, in_specs=[pl.BlockSpec(memory_space=pltpu.SM...  10.4 us
  transfers between devices with their start and end apart: 28, of which 10 were waited for; matrix products, arithmetic and copies ran while one was open for 0% of the time, Pallas kernels for 14%

profile of v2, /device:TPU:1, one launch (start us, length us, event | category | flops | bytes accessed | tf_op | source)
XLA Modules:
  0.0 305.2 jit_solution(1701361442417220993)
XLA Ops:
  0.0 8.8 %pack.1 = (bf16[8,104,512]{2,1,0:T(8,128)(2,1)}, bf16[8,1,104,512]{3,2,1,0:T(8,128)(2,1)}, bf16[8,1,104,512]{3,2,1,0:T(8,128)(2,1)}, bf16[8,1,104,512]{3,2,1,0:T...) custom-call(f32[8,96,512]{2,1,0:T(8,128)} %state.3, bf16[8,8,96,512]{3,2,1,0:T(8,128)(2,1)} %noise.3, ...), custom_call_target="tpu_custom_call" | custom-call | flops 1000000000 | bytes 14000000 | tf_op jit(solution)/shard_map/pack/pallas_call | solution.py:127
  8.8 21.2 %all_to_all.45.refs_5_.noise = bf16[8,104,512]{2,1,0:T(8,128)(2,1)} all-to-all(bf16[8,104,512]{2,1,0:T(8,128)(2,1)} %get-tuple-element.52), channel_id=1, replica_groups={{0,8,16,24,32,40,48,56},{64,72,80,88,96,104,112,120},{128,136,144,152,1..., dimensions={0} | all-to-all | bytes 1703936 | tf_op jit(solution)/shard_map/all_to_all | solution.py:449
  30.0 16.7 %all_to_all.46.refs_5_.noise = bf16[8,1,104,512]{3,2,1,0:T(8,128)(2,1)} all-to-all(bf16[8,1,104,512]{3,2,1,0:T(8,128)(2,1)S(1)} %copy-done.62), channel_id=1, replica_groups={{0,8,16,24,32,40,48,56},{64,72,80,88,96,104,112,120},{128,136,144,152,1..., dimensions={0} | all-to-all | bytes 1703936 | tf_op jit(solution)/shard_map/all_to_all | solution.py:449
  46.7 16.6 %all_to_all.47.refs_5_.noise = bf16[8,1,104,512]{3,2,1,0:T(8,128)(2,1)} all-to-all(bf16[8,1,104,512]{3,2,1,0:T(8,128)(2,1)S(1)} %copy-done.61), channel_id=1, replica_groups={{0,8,16,24,32,40,48,56},{64,72,80,88,96,104,112,120},{128,136,144,152,1..., dimensions={0} | all-to-all | bytes 1703936 | tf_op jit(solution)/shard_map/all_to_all | solution.py:449
  63.3 4.6 %all-to-all-start.4 = ((bf16[8,1,104,512]{3,2,1,0:T(8,128)(2,1)}), bf16[8,1,104,512]{3,2,1,0:T(8,128)(2,1)S(1)}, u32[]{:S(2)}, u32[]{:S(2)}) async-start(bf16[8,1,104,512]{3,2,1,0:T(8,128)(2,1)} %get-tuple-element.66), calls=%async_computation.4 | async-start | bytes 1703936 | tf_op jit(solution)/shard_map/all_to_all | solution.py:449
  67.9 4.1 %prep.1 = bf16[8,128,512]{2,1,0:T(8,128)(2,1)} custom-call(f32[8,96,512]{2,1,0:T(8,128)} %state.3, bf16[8,8,96,512]{3,2,1,0:T(8,128)(2,1)} %noise.3, f32[16,96]{1,0:T(8,128)} %weight.1, s32[16,96]{1,0:T(8,128)} %index.1, s32[1,8]{1,0:T(1,128)} %bound.3, s32[1,64]{1,0:T(1,128)} %observed.1, f32[1,64]{1,0:T(1,128)} %value.1, f32[1,64]{1,0:T(1,128)} %var.3, ...), custom_call_target="tpu_custom_call" | custom-call | tf_op jit(solution)/shard_map/prep/pallas_call | solution.py:88
  72.0 7.9 %all-to-all-done.4.refs_5_.noise = bf16[8,1,104,512]{3,2,1,0:T(8,128)(2,1)S(1)} async-done(((bf16[8,1,104,512]{3,2,1,0:T(8,128)(2,1)}), bf16[8,1,104,512]{3,2,1,0:T(8,128)(2,1)S(1)}, u32[]{:S(2)}, u32[]{:S(2)}) %all-to-all-start.4) | async-done | bytes 852000 | tf_op jit(solution)/shard_map/all_to_all | solution.py:449
  79.9 19.5 %all_to_all.48.slab.refs_0_.noise.extra = bf16[8,128,512]{2,1,0:T(8,128)(2,1)S(1)} all-to-all(bf16[8,128,512]{2,1,0:T(8,128)(2,1)} %prep.1), channel_id=1, replica_groups={{0,8,16,24,32,40,48,56},{64,72,80,88,96,104,112,120},{128,136,144,152,1..., dimensions={0} | all-to-all | bytes 2097152 | tf_op jit(solution)/shard_map/all_to_all | solution.py:449
  99.4 26.5 %all_to_all.49.refs_5_.noise = bf16[8,2,104,512]{3,2,1,0:T(8,128)(2,1)} all-to-all(bf16[8,2,104,512]{3,2,1,0:T(8,128)(2,1)S(1)} %copy-done.60), channel_id=1, replica_groups={{0,8,16,24,32,40,48,56},{64,72,80,88,96,104,112,120},{128,136,144,152,1..., dimensions={0} | all-to-all | bytes 3407872 | tf_op jit(solution)/shard_map/all_to_all | solution.py:449
  126.0 5.0 %all-to-all-start.6 = ((bf16[8,2,104,512]{3,2,1,0:T(8,128)(2,1)}), bf16[8,2,104,512]{3,2,1,0:T(8,128)(2,1)}, u32[]{:S(2)}, u32[]{:S(2)}) async-start(bf16[8,2,104,512]{3,2,1,0:T(8,128)(2,1)} %get-tuple-element.83), calls=%async_computation.6 | async-start | bytes 3407872 | tf_op jit(solution)/shard_map/all_to_all | solution.py:449
  131.7 6.5 %collective-permute-start.1 = (bf16[64,512]{1,0:T(8,128)(2,1)S(1)}, bf16[64,512]{1,0:T(8,128)(2,1)S(1)}, u32[]{:S(2)}, u32[]{:S(2)}) collective-permute-start(bf16[64,512]{1,0:T(8,128)(2,1)S(1)} %slice_bitcast_fusion.refs_6_.r0), channel_id=1, source_target_pairs={{0,128},{32,160},{64,192},{96,224},{128,0},{160,32},{192,64},{224,... | collective-permute-start | bytes 196616 | tf_op jit(solution)/shard_map/ppermute | solution.py:505
  140.5 4.1 %tables.1 = (bf16[8,96,96]{2,1,0:T(8,128)(2,1)S(1)}, bf16[8,96,256]{2,1,0:T(8,128)(2,1)S(1)}, bf16[8,16,96]{2,1,0:T(8,128)(2,1)S(1)}, bf16[64,256]{1,0:T(8,128)(2,1)S(1)}, f32[64,512]{1,0:T(8,128)S(1)}) custom-call(bf16[8,128,512]{2,1,0:T(8,128)(2,1)S(1)} %all_to_all.48.slab.refs_0_.noise.extra, s32[8,1,128]{2,1,0:T(1,128)S(1)} %copy.20.colmap), custom_call_target="tpu_custom_call" | custom-call | flops 1000000000 | bytes 10000000 | tf_op jit(solution)/shard_map/tables/pallas_call | solution.py:168
  149.5 7.2 %collective-permute-start.4 = (bf16[64,512]{1,0:T(8,128)(2,1)S(1)}, bf16[64,512]{1,0:T(8,128)(2,1)S(1)}, u32[]{:S(2)}, u32[]{:S(2)}) collective-permute-start(bf16[64,512]{1,0:T(8,128)(2,1)S(1)} %get-tuple-element.58.refs_7_.r0), channel_id=1, source_target_pairs={{0,128},{32,160},{64,192},{96,224},{128,0},{160,32},{192,64},{224,... | collective-permute-start | bytes 196616 | tf_op jit(solution)/shard_map/ppermute | solution.py:505
  168.6 4.5 %step.8 = (f32[8,96,512]{2,1,0:T(8,128)}, bf16[8,96,512]{2,1,0:T(8,128)(2,1)}, f32[64,512]{1,0:T(8,128)}) custom-call(bf16[8,96,512]{2,1,0:T(8,128)(2,1)} %get-tuple-element.53.refs_0_, bf16[8,96,96]{2,1,0:T(8,128)(2,1)} %copy-done.22, bf16[8,96,256]{2,1,0:T(8,128)(2,1)} %copy-done.19, bf16[8,16,96]{2,1,0:T(8,128)(2,1)} %copy-done.59, bf16[512,512]{1,0:T(8,128)(2,1)} %w.15, ...), custom_call_target="tpu_custom_call" | custom-call | flops 2000000000 | bytes 6000000 | tf_op jit(solution)/shard_map/step/pallas_call | solution.py:287
  180.7 4.4 %step.9 = (f32[8,96,512]{2,1,0:T(8,128)}, bf16[8,96,512]{2,1,0:T(8,128)(2,1)}, f32[64,512]{1,0:T(8,128)}) custom-call(bf16[8,96,512]{2,1,0:T(8,128)(2,1)} %get-tuple-element.59.refs_0_, bf16[8,96,96]{2,1,0:T(8,128)(2,1)} %copy-done.22, bf16[8,96,256]{2,1,0:T(8,128)(2,1)} %copy-done.19, bf16[8,16,96]{2,1,0:T(8,128)(2,1)} %copy-done.59, bf16[512,512]{1,0:T(8,128)(2,1)} %w.15, ...), custom_call_target="tpu_custom_call" | custom-call | flops 2000000000 | bytes 6000000 | tf_op jit(solution)/shard_map/step/pallas_call | solution.py:287
  192.4 4.4 %step.10 = (f32[8,96,512]{2,1,0:T(8,128)}, bf16[8,96,512]{2,1,0:T(8,128)(2,1)}, f32[64,512]{1,0:T(8,128)}) custom-call(bf16[8,96,512]{2,1,0:T(8,128)(2,1)} %get-tuple-element.65.refs_0_, bf16[8,96,96]{2,1,0:T(8,128)(2,1)} %copy-done.22, bf16[8,96,256]{2,1,0:T(8,128)(2,1)} %copy-done.19, bf16[8,16,96]{2,1,0:T(8,128)(2,1)} %copy-done.59, bf16[512,512]{1,0:T(8,128)(2,1)} %w.15, ...), custom_call_target="tpu_custom_call" | custom-call | flops 2000000000 | bytes 6000000 | tf_op jit(solution)/shard_map/step/pallas_call | solution.py:287
  205.0 4.4 %step.11 = (f32[8,96,512]{2,1,0:T(8,128)}, bf16[8,96,512]{2,1,0:T(8,128)(2,1)}, f32[64,512]{1,0:T(8,128)}) custom-call(bf16[8,96,512]{2,1,0:T(8,128)(2,1)} %get-tuple-element.71.refs_0_, bf16[8,96,96]{2,1,0:T(8,128)(2,1)} %copy-done.22, bf16[8,96,256]{2,1,0:T(8,128)(2,1)} %copy-done.19, bf16[8,16,96]{2,1,0:T(8,128)(2,1)} %copy-done.59, bf16[512,512]{1,0:T(8,128)(2,1)} %w.15, ...), custom_call_target="tpu_custom_call" | custom-call | flops 2000000000 | bytes 6000000 | tf_op jit(solution)/shard_map/step/pallas_call | solution.py:287
  216.7 4.5 %step.12 = (f32[8,96,512]{2,1,0:T(8,128)}, bf16[8,96,512]{2,1,0:T(8,128)(2,1)}, f32[64,512]{1,0:T(8,128)}) custom-call(bf16[8,96,512]{2,1,0:T(8,128)(2,1)} %get-tuple-element.77.refs_0_, bf16[8,96,96]{2,1,0:T(8,128)(2,1)} %copy-done.22, bf16[8,96,256]{2,1,0:T(8,128)(2,1)} %copy-done.19, bf16[8,16,96]{2,1,0:T(8,128)(2,1)} %copy-done.59, bf16[512,512]{1,0:T(8,128)(2,1)} %w.15, ...), custom_call_target="tpu_custom_call" | custom-call | flops 2000000000 | bytes 6000000 | tf_op jit(solution)/shard_map/step/pallas_call | solution.py:287
  230.0 4.4 %step.13 = (f32[8,96,512]{2,1,0:T(8,128)}, bf16[8,96,512]{2,1,0:T(8,128)(2,1)}, f32[64,512]{1,0:T(8,128)}) custom-call(bf16[8,96,512]{2,1,0:T(8,128)(2,1)} %get-tuple-element.82.refs_0_, bf16[8,96,96]{2,1,0:T(8,128)(2,1)} %copy-done.22, bf16[8,96,256]{2,1,0:T(8,128)(2,1)} %copy-done.19, bf16[8,16,96]{2,1,0:T(8,128)(2,1)} %copy-done.59, bf16[512,512]{1,0:T(8,128)(2,1)} %w.15, ...), custom_call_target="tpu_custom_call" | custom-call | flops 2000000000 | bytes 6000000 | tf_op jit(solution)/shard_map/step/pallas_call | solution.py:287
  243.6 7.5 %all-to-all-start.7 = ((bf16[32,2,56,128]{3,2,1,0:T(8,128)(2,1)}), bf16[32,2,56,128]{3,2,1,0:T(8,128)(2,1)S(1)}, u32[]{:S(2)}, u32[]{:S(2)}) async-start(bf16[32,2,56,128]{3,2,1,0:T(8,128)(2,1)} %bitcast.5), calls=%async_computation.7 | async-start | bytes 1835008 | tf_op jit(solution)/shard_map/all_to_all | solution.py:449
  251.2 10.5 %all-to-all-done.7 = bf16[32,2,56,128]{3,2,1,0:T(8,128)(2,1)S(1)} async-done(((bf16[32,2,56,128]{3,2,1,0:T(8,128)(2,1)}), bf16[32,2,56,128]{3,2,1,0:T(8,128)(2,1)S(1)}, u32[]{:S(2)}, u32[]{:S(2)}) %all-to-all-start.7) | async-done | bytes 917536 | tf_op jit(solution)/shard_map/all_to_all | solution.py:449
  261.8 14.9 %collective-permute-start.24 = (bf16[32,56,128]{2,1,0:T(8,128)(2,1)S(1)}, bf16[32,56,128]{2,1,0:T(8,128)(2,1)S(1)}, u32[]{:S(2)}, u32[]{:S(2)}) collective-permute-start(bf16[32,56,128]{2,1,0:T(8,128)(2,1)S(1)} %get-tuple-element.93), channel_id=1, source_target_pairs={{0,1},{1,0},{2,3},{3,2},{4,5},{5,4},{6,7},{7,6},{8,9},{9,8},{10,11... | collective-permute-start | bytes 1376264 | tf_op jit(solution)/shard_map/ppermute | solution.py:527
  278.2 10.4 %analyse.1 = bf16[8,8,48,128]{3,2,1,0:T(8,128)(2,1)S(1)} custom-call(s32[1]{0:T(128)} %bitcast.core, bf16[32,56,128]{2,1,0:T(8,128)(2,1)S(1)} %get-tuple-element.94.kept, bf16[32,56,128]{2,1,0:T(8,128)(2,1)S(1)} %collective-permute-done.24.other, f32[1,64]{1,0:T(1,128)S(1)} %copy-done.57), custom_call_target="tpu_custom_call" | custom-call | tf_op jit(solution)/shard_map/analyse/pallas_call | solution.py:391
  288.6 15.4 %all_to_all.50.data = bf16[8,8,48,128]{3,2,1,0:T(8,128)(2,1)S(1)} all-to-all(bf16[8,8,48,128]{3,2,1,0:T(8,128)(2,1)S(1)} %analyse.1), channel_id=1, replica_groups=mesh['z'=8,'y'=4,'x'=4,'core'=2] {'x','core'}, dimensions={0} | all-to-all | bytes 1572864 | tf_op jit(solution)/shard_map/all_to_all | solution.py:449
  (195 shorter events, 70.3 us)
Async XLA Ops:
  63.3 16.6 %all-to-all-start.4 = ((bf16[8,1,104,512]{3,2,1,0:T(8,128)(2,1)}), bf16[8,1,104,512]{3,2,1,0:T(8,128)(2,1)S(1)}, u32[]{:S(2)}, u32[]{:S(2)}) async-start(bf16[8,1,104,512]{3,2,1,0:T(8,128)(2,1)} %get-tuple-element.66), calls=%async_computation.4 | async-start | bytes 1703936 | tf_op jit(solution)/shard_map/all_to_all | solution.py:449
  126.0 104.0 %all-to-all-start.6 = ((bf16[8,2,104,512]{3,2,1,0:T(8,128)(2,1)}), bf16[8,2,104,512]{3,2,1,0:T(8,128)(2,1)}, u32[]{:S(2)}, u32[]{:S(2)}) async-start(bf16[8,2,104,512]{3,2,1,0:T(8,128)(2,1)} %get-tuple-element.83), calls=%async_computation.6 | async-start | bytes 3407872 | tf_op jit(solution)/shard_map/all_to_all | solution.py:449
  131.6 14.3 %collective-permute-start.2 = (bf16[64,512]{1,0:T(8,128)(2,1)S(1)}, bf16[64,512]{1,0:T(8,128)(2,1)S(1)}, u32[]{:S(2)}, u32[]{:S(2)}) collective-permute-start(bf16[64,512]{1,0:T(8,128)(2,1)S(1)} %slice_bitcast_fusion.refs_6_.r0), channel_id=1, source_target_pairs={{0,192},{32,224},{64,0},{96,32},{128,64},{160,96},{192,128},{224,1... | collective-permute-start | bytes 196616 | tf_op jit(solution)/shard_map/ppermute | solution.py:505
  131.7 14.2 %collective-permute-start.1 = (bf16[64,512]{1,0:T(8,128)(2,1)S(1)}, bf16[64,512]{1,0:T(8,128)(2,1)S(1)}, u32[]{:S(2)}, u32[]{:S(2)}) collective-permute-start(bf16[64,512]{1,0:T(8,128)(2,1)S(1)} %slice_bitcast_fusion.refs_6_.r0), channel_id=1, source_target_pairs={{0,128},{32,160},{64,192},{96,224},{128,0},{160,32},{192,64},{224,... | collective-permute-start | bytes 196616 | tf_op jit(solution)/shard_map/ppermute | solution.py:505
  138.2 7.7 %collective-permute-start = (bf16[64,512]{1,0:T(8,128)(2,1)S(1)}, bf16[64,512]{1,0:T(8,128)(2,1)S(1)}, u32[]{:S(2)}, u32[]{:S(2)}) collective-permute-start(bf16[64,512]{1,0:T(8,128)(2,1)S(1)} %slice_bitcast_fusion.refs_6_.r0), channel_id=1, source_target_pairs={{0,64},{32,96},{64,128},{96,160},{128,192},{160,224},{192,0},{224,... | collective-permute-start | bytes 196616 | tf_op jit(solution)/shard_map/ppermute | solution.py:505
  146.3 14.5 %collective-permute-start.5 = (bf16[64,512]{1,0:T(8,128)(2,1)S(1)}, bf16[64,512]{1,0:T(8,128)(2,1)S(1)}, u32[]{:S(2)}, u32[]{:S(2)}) collective-permute-start(bf16[64,512]{1,0:T(8,128)(2,1)S(1)} %get-tuple-element.58.refs_7_.r0), channel_id=1, source_target_pairs={{0,192},{32,224},{64,0},{96,32},{128,64},{160,96},{192,128},{224,1... | collective-permute-start | bytes 196616 | tf_op jit(solution)/shard_map/ppermute | solution.py:505
  149.5 11.3 %collective-permute-start.4 = (bf16[64,512]{1,0:T(8,128)(2,1)S(1)}, bf16[64,512]{1,0:T(8,128)(2,1)S(1)}, u32[]{:S(2)}, u32[]{:S(2)}) collective-permute-start(bf16[64,512]{1,0:T(8,128)(2,1)S(1)} %get-tuple-element.58.refs_7_.r0), channel_id=1, source_target_pairs={{0,128},{32,160},{64,192},{96,224},{128,0},{160,32},{192,64},{224,... | collective-permute-start | bytes 196616 | tf_op jit(solution)/shard_map/ppermute | solution.py:505
  163.8 9.2 %collective-permute-start.8 = (bf16[64,512]{1,0:T(8,128)(2,1)S(1)}, bf16[64,512]{1,0:T(8,128)(2,1)S(1)}, u32[]{:S(2)}, u32[]{:S(2)}) collective-permute-start(bf16[64,512]{1,0:T(8,128)(2,1)S(1)} %get-tuple-element.64.refs_7_.r0), channel_id=1, source_target_pairs={{0,192},{32,224},{64,0},{96,32},{128,64},{160,96},{192,128},{224,1... | collective-permute-start | bytes 196616 | tf_op jit(solution)/shard_map/ppermute | solution.py:505
  165.8 7.9 %collective-permute-start.7 = (bf16[64,512]{1,0:T(8,128)(2,1)S(1)}, bf16[64,512]{1,0:T(8,128)(2,1)S(1)}, u32[]{:S(2)}, u32[]{:S(2)}) collective-permute-start(bf16[64,512]{1,0:T(8,128)(2,1)S(1)} %get-tuple-element.64.refs_7_.r0), channel_id=1, source_target_pairs={{0,128},{32,160},{64,192},{96,224},{128,0},{160,32},{192,64},{224,... | collective-permute-start | bytes 196616 | tf_op jit(solution)/shard_map/ppermute | solution.py:505
  175.0 10.1 %collective-permute-start.11 = (bf16[64,512]{1,0:T(8,128)(2,1)S(1)}, bf16[64,512]{1,0:T(8,128)(2,1)S(1)}, u32[]{:S(2)}, u32[]{:S(2)}) collective-permute-start(bf16[64,512]{1,0:T(8,128)(2,1)S(1)} %get-tuple-element.70.refs_7_.r0), channel_id=1, source_target_pairs={{0,192},{32,224},{64,0},{96,32},{128,64},{160,96},{192,128},{224,1... | collective-permute-start | bytes 196616 | tf_op jit(solution)/shard_map/ppermute | solution.py:505
  176.6 8.5 %collective-permute-start.10 = (bf16[64,512]{1,0:T(8,128)(2,1)S(1)}, bf16[64,512]{1,0:T(8,128)(2,1)S(1)}, u32[]{:S(2)}, u32[]{:S(2)}) collective-permute-start(bf16[64,512]{1,0:T(8,128)(2,1)S(1)} %get-tuple-element.70.refs_7_.r0), channel_id=1, source_target_pairs={{0,128},{32,160},{64,192},{96,224},{128,0},{160,32},{192,64},{224,... | collective-permute-start | bytes 196616 | tf_op jit(solution)/shard_map/ppermute | solution.py:505
  187.2 9.6 %collective-permute-start.14 = (bf16[64,512]{1,0:T(8,128)(2,1)S(1)}, bf16[64,512]{1,0:T(8,128)(2,1)S(1)}, u32[]{:S(2)}, u32[]{:S(2)}) collective-permute-start(bf16[64,512]{1,0:T(8,128)(2,1)S(1)} %get-tuple-element.76.refs_7_.r0), channel_id=1, source_target_pairs={{0,192},{32,224},{64,0},{96,32},{128,64},{160,96},{192,128},{224,1... | collective-permute-start | bytes 196616 | tf_op jit(solution)/shard_map/ppermute | solution.py:505
  190.1 8.1 %collective-permute-start.13 = (bf16[64,512]{1,0:T(8,128)(2,1)S(1)}, bf16[64,512]{1,0:T(8,128)(2,1)S(1)}, u32[]{:S(2)}, u32[]{:S(2)}) collective-permute-start(bf16[64,512]{1,0:T(8,128)(2,1)S(1)} %get-tuple-element.76.refs_7_.r0), channel_id=1, source_target_pairs={{0,128},{32,160},{64,192},{96,224},{128,0},{160,32},{192,64},{224,... | collective-permute-start | bytes 196616 | tf_op jit(solution)/shard_map/ppermute | solution.py:505
  191.5 6.8 %collective-permute-start.12 = (bf16[64,512]{1,0:T(8,128)(2,1)S(1)}, bf16[64,512]{1,0:T(8,128)(2,1)S(1)}, u32[]{:S(2)}, u32[]{:S(2)}) collective-permute-start(bf16[64,512]{1,0:T(8,128)(2,1)S(1)} %get-tuple-element.76.refs_7_.r0), channel_id=1, source_target_pairs={{0,64},{32,96},{64,128},{96,160},{128,192},{160,224},{192,0},{224,... | collective-permute-start | bytes 196616 | tf_op jit(solution)/shard_map/ppermute | solution.py:505
  199.6 9.9 %collective-permute-start.17 = (bf16[64,512]{1,0:T(8,128)(2,1)S(1)}, bf16[64,512]{1,0:T(8,128)(2,1)S(1)}, u32[]{:S(2)}, u32[]{:S(2)}) collective-permute-start(bf16[64,512]{1,0:T(8,128)(2,1)S(1)} %get-tuple-element.81.refs_7_.r0), channel_id=1, source_target_pairs={{0,192},{32,224},{64,0},{96,32},{128,64},{160,96},{192,128},{224,1... | collective-permute-start | bytes 196616 | tf_op jit(solution)/shard_map/ppermute | solution.py:505
  200.9 8.5 %collective-permute-start.16 = (bf16[64,512]{1,0:T(8,128)(2,1)S(1)}, bf16[64,512]{1,0:T(8,128)(2,1)S(1)}, u32[]{:S(2)}, u32[]{:S(2)}) collective-permute-start(bf16[64,512]{1,0:T(8,128)(2,1)S(1)} %get-tuple-element.81.refs_7_.r0), channel_id=1, source_target_pairs={{0,128},{32,160},{64,192},{96,224},{128,0},{160,32},{192,64},{224,... | collective-permute-start | bytes 196616 | tf_op jit(solution)/shard_map/ppermute | solution.py:505
  211.5 9.7 %collective-permute-start.20 = (bf16[64,512]{1,0:T(8,128)(2,1)S(1)}, bf16[64,512]{1,0:T(8,128)(2,1)S(1)}, u32[]{:S(2)}, u32[]{:S(2)}) collective-permute-start(bf16[64,512]{1,0:T(8,128)(2,1)S(1)} %get-tuple-element.87.refs_7_.r0), channel_id=1, source_target_pairs={{0,192},{32,224},{64,0},{96,32},{128,64},{160,96},{192,128},{224,1... | collective-permute-start | bytes 196616 | tf_op jit(solution)/shard_map/ppermute | solution.py:505
  214.5 9.3 %collective-permute-start.19 = (bf16[64,512]{1,0:T(8,128)(2,1)S(1)}, bf16[64,512]{1,0:T(8,128)(2,1)S(1)}, u32[]{:S(2)}, u32[]{:S(2)}) collective-permute-start(bf16[64,512]{1,0:T(8,128)(2,1)S(1)} %get-tuple-element.87.refs_7_.r0), channel_id=1, source_target_pairs={{0,128},{32,160},{64,192},{96,224},{128,0},{160,32},{192,64},{224,... | collective-permute-start | bytes 196616 | tf_op jit(solution)/shard_map/ppermute | solution.py:505
  215.8 7.9 %collective-permute-start.18 = (bf16[64,512]{1,0:T(8,128)(2,1)S(1)}, bf16[64,512]{1,0:T(8,128)(2,1)S(1)}, u32[]{:S(2)}, u32[]{:S(2)}) collective-permute-start(bf16[64,512]{1,0:T(8,128)(2,1)S(1)} %get-tuple-element.87.refs_7_.r0), channel_id=1, source_target_pairs={{0,64},{32,96},{64,128},{96,160},{128,192},{160,224},{192,0},{224,... | collective-permute-start | bytes 196616 | tf_op jit(solution)/shard_map/ppermute | solution.py:505
  225.7 8.8 %collective-permute-start.23 = (bf16[64,512]{1,0:T(8,128)(2,1)S(1)}, bf16[64,512]{1,0:T(8,128)(2,1)S(1)}, u32[]{:S(2)}, u32[]{:S(2)}) collective-permute-start(bf16[64,512]{1,0:T(8,128)(2,1)S(1)} %get-tuple-element.92.r0), channel_id=1, source_target_pairs={{0,192},{32,224},{64,0},{96,32},{128,64},{160,96},{192,128},{224,1... | collective-permute-start | bytes 196616 | tf_op jit(solution)/shard_map/ppermute | solution.py:505
  226.8 10.7 %collective-permute-start.22 = (bf16[64,512]{1,0:T(8,128)(2,1)S(1)}, bf16[64,512]{1,0:T(8,128)(2,1)S(1)}, u32[]{:S(2)}, u32[]{:S(2)}) collective-permute-start(bf16[64,512]{1,0:T(8,128)(2,1)S(1)} %get-tuple-element.92.r0), channel_id=1, source_target_pairs={{0,128},{32,160},{64,192},{96,224},{128,0},{160,32},{192,64},{224,... | collective-permute-start | bytes 196616 | tf_op jit(solution)/shard_map/ppermute | solution.py:505
  229.9 7.6 %collective-permute-start.21 = (bf16[64,512]{1,0:T(8,128)(2,1)S(1)}, bf16[64,512]{1,0:T(8,128)(2,1)S(1)}, u32[]{:S(2)}, u32[]{:S(2)}) collective-permute-start(bf16[64,512]{1,0:T(8,128)(2,1)S(1)} %get-tuple-element.92.r0), channel_id=1, source_target_pairs={{0,64},{32,96},{64,128},{96,160},{128,192},{160,224},{192,0},{224,... | collective-permute-start | bytes 196616 | tf_op jit(solution)/shard_map/ppermute | solution.py:505
  243.6 18.1 %all-to-all-start.7 = ((bf16[32,2,56,128]{3,2,1,0:T(8,128)(2,1)}), bf16[32,2,56,128]{3,2,1,0:T(8,128)(2,1)S(1)}, u32[]{:S(2)}, u32[]{:S(2)}) async-start(bf16[32,2,56,128]{3,2,1,0:T(8,128)(2,1)} %bitcast.5), calls=%async_computation.7 | async-start | bytes 1835008 | tf_op jit(solution)/shard_map/all_to_all | solution.py:449
  261.8 16.4 %collective-permute-start.24 = (bf16[32,56,128]{2,1,0:T(8,128)(2,1)S(1)}, bf16[32,56,128]{2,1,0:T(8,128)(2,1)S(1)}, u32[]{:S(2)}, u32[]{:S(2)}) collective-permute-start(bf16[32,56,128]{2,1,0:T(8,128)(2,1)S(1)} %get-tuple-element.93), channel_id=1, source_target_pairs={{0,1},{1,0},{2,3},{3,2},{4,5},{5,4},{6,7},{7,6},{8,9},{9,8},{10,11... | collective-permute-start | bytes 1376264 | tf_op jit(solution)/shard_map/ppermute | solution.py:527
  (68 other events, 620.2 us)

commit v3 on v2

--- a/solution.py
+++ b/solution.py
@@ -60,7 +60,7 @@
 
 def prep_body(state, noise, weight, index, bound, observed, value, var, pert, slab):
     chosen = chosen_rows(bound[...])
-    for j in range(2):
+    for j in range(4):
         rate = jnp.tanh(state[j]).astype(BF)
         slab[j, 0:VOX, :] = rate
         slab[j, VOX : VOX + AUX, :] = jnp.zeros((AUX, STATE), BF)
@@ -87,19 +87,19 @@
 def prep(state, noise, weight, index, bound, observed, value, var, pert):
     return pl.pallas_call(
         prep_body,
-        grid=(PARTS // 2,),
+        grid=(PARTS // 4,),
         in_specs=[
-            pl.BlockSpec((2, VOX, STATE), lambda j: (j, 0, 0)),
-            pl.BlockSpec((1, 2, VOX, STATE), lambda j: (0, j, 0, 0)),
+            pl.BlockSpec((4, VOX, STATE), lambda j: (j, 0, 0)),
+            pl.BlockSpec((1, 4, VOX, STATE), lambda j: (0, j, 0, 0)),
             whole(KIN, VOX),
             whole(KIN, VOX),
             whole(1, BND),
             whole(1, OBS),
             whole(1, OBS),
             whole(1, OBS),
-            pl.BlockSpec((2, 1, OBS), lambda j: (j, 0, 0)),
-        ],
-        out_specs=pl.BlockSpec((2, VOX + 2 * AUX, STATE), lambda j: (j, 0, 0)),
+            pl.BlockSpec((4, 1, OBS), lambda j: (j, 0, 0)),
+        ],
+        out_specs=pl.BlockSpec((4, VOX + 2 * AUX, STATE), lambda j: (j, 0, 0)),
         out_shape=jax.ShapeDtypeStruct((PARTS, VOX + 2 * AUX, STATE), BF),
         name="prep",
     )(state, noise, weight, index, bound, observed, value, var, pert)
@@ -118,7 +118,7 @@
             out[0, place, VOX:, :] = found[t]
 
 
-BATCHES = ((1,), (2,), (3,), (4, 5), (6, 7))
+BATCHES = ((1,), (2,), (3,), (4,), (5,), (6, 7))
 FIRST = VOX + BND
 
 
@@ -338,7 +338,6 @@
         out_specs=pl.BlockSpec((GROUP * 8, CHUNK + TAIL, 128), lambda q: (q, 0, 0)),
         out_shape=jax.ShapeDtypeStruct((PARTS * 8, CHUNK + TAIL, 128), BF),
         name="last",
-        compiler_params=SMALL,
         cost_estimate=STEP_COST,
     )(rate, own, halo, w, noise, current, *table, slab, readout)
 
@@ -358,15 +357,9 @@
     covar = covar + jnp.where(iota(square, 0) == iota(square, 1), var[...], 0.0)
     work = jnp.concatenate([covar, flipped], axis=1)
     row = iota((OBS, 2 * OBS), 0)
-    for k in range(0, OBS, 2):
-        upper, lower = work[k : k + 1, :], work[k + 1 : k + 2, :]
-        a, b = upper[:, k : k + 1], upper[:, k + 1 : k + 2]
-        c, d = lower[:, k : k + 1], lower[:, k + 1 : k + 2]
-        scale = 1.0 / (a * d - b * c)
-        one = (d * upper - b * lower) * scale
-        two = (a * lower - c * upper) * scale
-        rest = work - work[:, k : k + 1] * one - work[:, k + 1 : k + 2] * two
-        work = jnp.where(row == k, one, jnp.where(row == k + 1, two, rest))
+    for k in range(OBS):
+        pivot = work[k : k + 1, :] / work[k : k + 1, k : k + 1]
+        work = jnp.where(row == k, pivot, work - work[:, k : k + 1] * pivot)
     solved = work[:, OBS : 2 * OBS]
     mixing = jnp.dot(innov, solved, precision=HIGH, preferred_element_type=F32) / (MEMBERS - 1)
     mixing = mixing - jnp.mean(mixing, axis=1, keepdims=True)

time: 306 us -> 313 us (1.023)
  starting transfers between devices: 81.7 us -> 89.3 us
  blocking collectives: 116 us -> 122 us
    all_to_all x6 -> x7, blocking collectives: 116 us -> 122 us  [swap(): lax.all_to_all(value, axes, split_axis=0, concat_axis=0, tiled=True, axis...]
    ppermute x24, waiting for transfers between devices: 10.8 us -> 6.78 us  [per_device(): lax.ppermute(edge_rate, 'z', [(i, (i + 2 * o) % DEPTH) for i in range(DEP...]
    all_to_all x3, starting transfers between devices: 17.2 us -> 21 us  [swap(): lax.all_to_all(value, axes, split_axis=0, concat_axis=0, tiled=True, axis...]
    ppermute x24, starting transfers between devices: 49.6 us -> 53.2 us  [per_device(): lax.ppermute(edge_rate, 'z', [(i, (i + 2 * o) % DEPTH) for i in range(DEP...]
    unnamed x130 -> x126, local copies, waits for them, and re-layouts: 9.85 us -> 7.9 us
  transfers between devices with their start and end apart: 28 -> 28, of which waited for: 10 -> 11; matrix products, arithmetic and copies ran while one was open for 0% -> 0% of each run, Pallas kernels for 14% -> 13%
where the time goes in v3:
time: 313 us; the launch traced here: 312 us
  blocking collectives  122 us (39%)
  starting transfers between devices  89.3 us (29%)
  Pallas kernels  63.5 us (20%)
  waiting for transfers between devices  27.7 us (9%)
  local copies, waits for them, and re-layouts  8.28 us (3%)
    all_to_all x7, blocking collectives, swap(): lax.all_to_all(value, axes, split_axis=0, concat_axis=0, tiled=True, axis...  122 us
    ppermute x24, starting transfers between devices, per_device(): lax.ppermute(edge_rate, 'z', [(i, (i + 2 * o) % DEPTH) for i in range(DEP...  53.2 us
    pallas_call x7, Pallas kernels, step(): pl.pallas_call(functools.partial(step_body, current is not None), grid=(P...  30.5 us
    all_to_all x3, starting transfers between devices, swap(): lax.all_to_all(value, axes, split_axis=0, concat_axis=0, tiled=True, axis...  21 us
    all_to_all x3, waiting for transfers between devices, swap(): lax.all_to_all(value, axes, split_axis=0, concat_axis=0, tiled=True, axis...  19.5 us
    ppermute x1, starting transfers between devices, per_device(): other = lax.ppermute(other, 'core', [(0, 1), (1, 0)])  15.1 us
    pallas_call x1, Pallas kernels, pack(): pl.pallas_call(pack_body, grid=(PARTS,), in_specs=[pl.BlockSpec((1, VOX,...  8.82 us
    pallas_call x1, Pallas kernels, analyse(): pl.pallas_call(analyse_body, in_specs=[pl.BlockSpec(memory_space=pltpu.SM...  8.65 us
  transfers between devices with their start and end apart: 28, of which 11 were waited for; matrix products, arithmetic and copies ran while one was open for 0% of the time, Pallas kernels for 13%

profile of v3, /device:TPU:1, one launch (start us, length us, event | category | flops | bytes accessed | tf_op | source)
XLA Modules:
  0.0 311.6 jit_solution(5799895536089080202)
XLA Ops:
  0.0 8.8 %pack.1 = (bf16[8,104,512]{2,1,0:T(8,128)(2,1)}, bf16[8,1,104,512]{3,2,1,0:T(8,128)(2,1)}, bf16[8,1,104,512]{3,2,1,0:T(8,128)(2,1)}, bf16[8,1,104,512]{3,2,1,0:T...) custom-call(f32[8,96,512]{2,1,0:T(8,128)} %state.3, ...), custom_call_target="tpu_custom_call" | custom-call | flops 1000000000 | bytes 14000000 | tf_op jit(solution)/shard_map/pack/pallas_call | solution.py:127
  8.8 21.2 %all_to_all.50.refs_5_.noise = bf16[8,104,512]{2,1,0:T(8,128)(2,1)} all-to-all(bf16[8,104,512]{2,1,0:T(8,128)(2,1)} %get-tuple-element.53), channel_id=1, replica_groups={{0,8,16,24,32,40,48,56},{64,72,80,88,96,104,112,120},{128,136,144,152,1..., dimensions={0} | all-to-all | bytes 1703936 | tf_op jit(solution)/shard_map/all_to_all | solution.py:442
  30.0 16.8 %all_to_all.51.refs_5_.noise = bf16[8,1,104,512]{3,2,1,0:T(8,128)(2,1)} all-to-all(bf16[8,1,104,512]{3,2,1,0:T(8,128)(2,1)S(1)} %copy-done.57), channel_id=1, replica_groups={{0,8,16,24,32,40,48,56},{64,72,80,88,96,104,112,120},{128,136,144,152,1..., dimensions={0} | all-to-all | bytes 1703936 | tf_op jit(solution)/shard_map/all_to_all | solution.py:442
  46.8 16.7 %all_to_all.52.refs_5_.noise = bf16[8,1,104,512]{3,2,1,0:T(8,128)(2,1)} all-to-all(bf16[8,1,104,512]{3,2,1,0:T(8,128)(2,1)S(1)} %copy-done.56), channel_id=1, replica_groups={{0,8,16,24,32,40,48,56},{64,72,80,88,96,104,112,120},{128,136,144,152,1..., dimensions={0} | all-to-all | bytes 1703936 | tf_op jit(solution)/shard_map/all_to_all | solution.py:442
  63.5 16.4 %all_to_all.53.refs_5_.noise = bf16[8,1,104,512]{3,2,1,0:T(8,128)(2,1)} all-to-all(bf16[8,1,104,512]{3,2,1,0:T(8,128)(2,1)S(1)} %copy-done.55), channel_id=1, replica_groups={{0,8,16,24,32,40,48,56},{64,72,80,88,96,104,112,120},{128,136,144,152,1..., dimensions={0} | all-to-all | bytes 1703936 | tf_op jit(solution)/shard_map/all_to_all | solution.py:442
  80.0 16.3 %all_to_all.54.refs_5_.noise = bf16[8,1,104,512]{3,2,1,0:T(8,128)(2,1)} all-to-all(bf16[8,1,104,512]{3,2,1,0:T(8,128)(2,1)S(1)} %copy-done.54), channel_id=1, replica_groups={{0,8,16,24,32,40,48,56},{64,72,80,88,96,104,112,120},{128,136,144,152,1..., dimensions={0} | all-to-all | bytes 1703936 | tf_op jit(solution)/shard_map/all_to_all | solution.py:442
  96.3 4.6 %all-to-all-start.6 = ((bf16[8,1,104,512]{3,2,1,0:T(8,128)(2,1)}), bf16[8,1,104,512]{3,2,1,0:T(8,128)(2,1)S(1)}, u32[]{:S(2)}, u32[]{:S(2)}) async-start(bf16[8,1,104,512]{3,2,1,0:T(8,128)(2,1)} %get-tuple-element.79), calls=%async_computation.6 | async-start | bytes 1703936 | tf_op jit(solution)/shard_map/all_to_all | solution.py:442
  103.8 8.9 %all-to-all-done.6.refs_5_.noise = bf16[8,1,104,512]{3,2,1,0:T(8,128)(2,1)S(1)} async-done(((bf16[8,1,104,512]{3,2,1,0:T(8,128)(2,1)}), bf16[8,1,104,512]{3,2,1,0:T(8,128)(2,1)S(1)}, u32[]{:S(2)}, u32[]{:S(2)}) %all-to-all-start.6) | async-done | bytes 852000 | tf_op jit(solution)/shard_map/all_to_all | solution.py:442
  112.7 19.3 %all_to_all.55.slab.refs_0_.noise.extra = bf16[8,128,512]{2,1,0:T(8,128)(2,1)S(1)} all-to-all(bf16[8,128,512]{2,1,0:T(8,128)(2,1)} %prep.1), channel_id=1, replica_groups={{0,8,16,24,32,40,48,56},{64,72,80,88,96,104,112,120},{128,136,144,152,1..., dimensions={0} | all-to-all | bytes 2097152 | tf_op jit(solution)/shard_map/all_to_all | solution.py:442
  132.0 5.0 %all-to-all-start.7 = ((bf16[8,2,104,512]{3,2,1,0:T(8,128)(2,1)}), bf16[8,2,104,512]{3,2,1,0:T(8,128)(2,1)}, u32[]{:S(2)}, u32[]{:S(2)}) async-start(bf16[8,2,104,512]{3,2,1,0:T(8,128)(2,1)} %get-tuple-element.85), calls=%async_computation.7 | async-start | bytes 3407872 | tf_op jit(solution)/shard_map/all_to_all | solution.py:442
  137.7 7.8 %collective-permute-start.1 = (bf16[64,512]{1,0:T(8,128)(2,1)S(1)}, bf16[64,512]{1,0:T(8,128)(2,1)S(1)}, u32[]{:S(2)}, u32[]{:S(2)}) collective-permute-start(bf16[64,512]{1,0:T(8,128)(2,1)S(1)} %slice_bitcast_fusion.refs_6_.r0), channel_id=1, source_target_pairs={{0,128},{32,160},{64,192},{96,224},{128,0},{160,32},{192,64},{224,... | collective-permute-start | bytes 196616 | tf_op jit(solution)/shard_map/ppermute | solution.py:498
  155.7 8.0 %collective-permute-start.4 = (bf16[64,512]{1,0:T(8,128)(2,1)S(1)}, bf16[64,512]{1,0:T(8,128)(2,1)S(1)}, u32[]{:S(2)}, u32[]{:S(2)}) collective-permute-start(bf16[64,512]{1,0:T(8,128)(2,1)S(1)} %get-tuple-element.59.refs_7_.r0), channel_id=1, source_target_pairs={{0,128},{32,160},{64,192},{96,224},{128,0},{160,32},{192,64},{224,... | collective-permute-start | bytes 196616 | tf_op jit(solution)/shard_map/ppermute | solution.py:498
  175.1 4.4 %step.8 = (f32[8,96,512]{2,1,0:T(8,128)}, bf16[8,96,512]{2,1,0:T(8,128)(2,1)}, f32[64,512]{1,0:T(8,128)}) custom-call(bf16[8,96,512]{2,1,0:T(8,128)(2,1)} %get-tuple-element.54.refs_0_, bf16[8,96,96]{2,1,0:T(8,128)(2,1)} %copy-done.17, bf16[8,96,256]{2,1,0:T(8,128)(2,1)} %copy-done.15, bf16[8,16,96]{2,1,0:T(8,128)(2,1)} %copy-done.53, bf16[512,512]{1,0:T(8,128)(2,1)} %w.15, ...), custom_call_target="tpu_custom_call" | custom-call | flops 2000000000 | bytes 6000000 | tf_op jit(solution)/shard_map/step/pallas_call | solution.py:287
  187.7 4.4 %step.9 = (f32[8,96,512]{2,1,0:T(8,128)}, bf16[8,96,512]{2,1,0:T(8,128)(2,1)}, f32[64,512]{1,0:T(8,128)}) custom-call(bf16[8,96,512]{2,1,0:T(8,128)(2,1)} %get-tuple-element.60.refs_0_, bf16[8,96,96]{2,1,0:T(8,128)(2,1)} %copy-done.17, bf16[8,96,256]{2,1,0:T(8,128)(2,1)} %copy-done.15, bf16[8,16,96]{2,1,0:T(8,128)(2,1)} %copy-done.53, bf16[512,512]{1,0:T(8,128)(2,1)} %w.15, ...), custom_call_target="tpu_custom_call" | custom-call | flops 2000000000 | bytes 6000000 | tf_op jit(solution)/shard_map/step/pallas_call | solution.py:287
  199.9 4.5 %step.10 = (f32[8,96,512]{2,1,0:T(8,128)}, bf16[8,96,512]{2,1,0:T(8,128)(2,1)}, f32[64,512]{1,0:T(8,128)}) custom-call(bf16[8,96,512]{2,1,0:T(8,128)(2,1)} %get-tuple-element.66.refs_0_, bf16[8,96,96]{2,1,0:T(8,128)(2,1)} %copy-done.17, bf16[8,96,256]{2,1,0:T(8,128)(2,1)} %copy-done.15, bf16[8,16,96]{2,1,0:T(8,128)(2,1)} %copy-done.53, bf16[512,512]{1,0:T(8,128)(2,1)} %w.15, ...), custom_call_target="tpu_custom_call" | custom-call | flops 2000000000 | bytes 6000000 | tf_op jit(solution)/shard_map/step/pallas_call | solution.py:287
  212.0 4.4 %step.11 = (f32[8,96,512]{2,1,0:T(8,128)}, bf16[8,96,512]{2,1,0:T(8,128)(2,1)}, f32[64,512]{1,0:T(8,128)}) custom-call(bf16[8,96,512]{2,1,0:T(8,128)(2,1)} %get-tuple-element.72.refs_0_, bf16[8,96,96]{2,1,0:T(8,128)(2,1)} %copy-done.17, bf16[8,96,256]{2,1,0:T(8,128)(2,1)} %copy-done.15, bf16[8,16,96]{2,1,0:T(8,128)(2,1)} %copy-done.53, bf16[512,512]{1,0:T(8,128)(2,1)} %w.15, ...), custom_call_target="tpu_custom_call" | custom-call | flops 2000000000 | bytes 6000000 | tf_op jit(solution)/shard_map/step/pallas_call | solution.py:287
  224.7 4.5 %step.12 = (f32[8,96,512]{2,1,0:T(8,128)}, bf16[8,96,512]{2,1,0:T(8,128)(2,1)}, f32[64,512]{1,0:T(8,128)}) custom-call(bf16[8,96,512]{2,1,0:T(8,128)(2,1)} %get-tuple-element.78.refs_0_, bf16[8,96,96]{2,1,0:T(8,128)(2,1)} %copy-done.17, bf16[8,96,256]{2,1,0:T(8,128)(2,1)} %copy-done.15, bf16[8,16,96]{2,1,0:T(8,128)(2,1)} %copy-done.53, bf16[512,512]{1,0:T(8,128)(2,1)} %w.15, ...), custom_call_target="tpu_custom_call" | custom-call | flops 2000000000 | bytes 6000000 | tf_op jit(solution)/shard_map/step/pallas_call | solution.py:287
  237.9 4.3 %step.13 = (f32[8,96,512]{2,1,0:T(8,128)}, bf16[8,96,512]{2,1,0:T(8,128)(2,1)}, f32[64,512]{1,0:T(8,128)}) custom-call(bf16[8,96,512]{2,1,0:T(8,128)(2,1)} %get-tuple-element.84.refs_0_, bf16[8,96,96]{2,1,0:T(8,128)(2,1)} %copy-done.17, bf16[8,96,256]{2,1,0:T(8,128)(2,1)} %copy-done.15, bf16[8,16,96]{2,1,0:T(8,128)(2,1)} %copy-done.53, bf16[512,512]{1,0:T(8,128)(2,1)} %w.15, ...), custom_call_target="tpu_custom_call" | custom-call | flops 2000000000 | bytes 6000000 | tf_op jit(solution)/shard_map/step/pallas_call | solution.py:287
  243.5 4.3 %last.1 = bf16[64,56,128]{2,1,0:T(8,128)(2,1)} custom-call(bf16[8,96,512]{2,1,0:T(8,128)(2,1)} %get-tuple-element.90.rate, bf16[8,96,96]{2,1,0:T(8,128)(2,1)} %copy-done.17, bf16[8,96,256]{2,1,0:T(8,128)(2,1)} %copy-done.15, bf16[512,512]{1,0:T(8,128)(2,1)} %w.15, bf16[8,2,104,512]{3,2,1,0:T(8,128)(2,1)} %all-to-all-done.7.refs_5_.noise, ...), custom_call_target="tpu_custom_call" | custom-call | flops 2000000000 | bytes 6000000 | tf_op jit(solution)/shard_map/last/pallas_call | solution.py:330
  247.8 11.4 %all-to-all-start.8 = ((bf16[32,2,56,128]{3,2,1,0:T(8,128)(2,1)}), bf16[32,2,56,128]{3,2,1,0:T(8,128)(2,1)S(1)}, u32[]{:S(2)}, u32[]{:S(2)}) async-start(bf16[32,2,56,128]{3,2,1,0:T(8,128)(2,1)} %bitcast.12), calls=%async_computation.8 | async-start | bytes 1835008 | tf_op jit(solution)/shard_map/all_to_all | solution.py:442
  259.2 10.5 %all-to-all-done.8 = bf16[32,2,56,128]{3,2,1,0:T(8,128)(2,1)S(1)} async-done(((bf16[32,2,56,128]{3,2,1,0:T(8,128)(2,1)}), bf16[32,2,56,128]{3,2,1,0:T(8,128)(2,1)S(1)}, u32[]{:S(2)}, u32[]{:S(2)}) %all-to-all-start.8) | async-done | bytes 917536 | tf_op jit(solution)/shard_map/all_to_all | solution.py:442
  269.8 15.1 %collective-permute-start.24 = (bf16[32,56,128]{2,1,0:T(8,128)(2,1)S(1)}, bf16[32,56,128]{2,1,0:T(8,128)(2,1)S(1)}, u32[]{:S(2)}, u32[]{:S(2)}) collective-permute-start(bf16[32,56,128]{2,1,0:T(8,128)(2,1)S(1)} %get-tuple-element.95), channel_id=1, source_target_pairs={{0,1},{1,0},{2,3},{3,2},{4,5},{5,4},{6,7},{7,6},{8,9},{9,8},{10,11... | collective-permute-start | bytes 1376264 | tf_op jit(solution)/shard_map/ppermute | solution.py:520
  286.3 8.7 %analyse.1 = bf16[8,8,48,128]{3,2,1,0:T(8,128)(2,1)S(1)} custom-call(s32[1]{0:T(128)} %bitcast.core, bf16[32,56,128]{2,1,0:T(8,128)(2,1)S(1)} %get-tuple-element.96.kept, bf16[32,56,128]{2,1,0:T(8,128)(2,1)S(1)} %collective-permute-done.24.other, f32[1,64]{1,0:T(1,128)S(1)} %copy-done.52), custom_call_target="tpu_custom_call" | custom-call | tf_op jit(solution)/shard_map/analyse/pallas_call | solution.py:384
  295.0 15.4 %all_to_all.56.data = bf16[8,8,48,128]{3,2,1,0:T(8,128)(2,1)S(1)} all-to-all(bf16[8,8,48,128]{3,2,1,0:T(8,128)(2,1)S(1)} %analyse.1), channel_id=1, replica_groups=mesh['z'=8,'y'=4,'x'=4,'core'=2] {'x','core'}, dimensions={0} | all-to-all | bytes 1572864 | tf_op jit(solution)/shard_map/all_to_all | solution.py:442
  (192 shorter events, 69.2 us)
Async XLA Ops:
  96.3 16.4 %all-to-all-start.6 = ((bf16[8,1,104,512]{3,2,1,0:T(8,128)(2,1)}), bf16[8,1,104,512]{3,2,1,0:T(8,128)(2,1)S(1)}, u32[]{:S(2)}, u32[]{:S(2)}) async-start(bf16[8,1,104,512]{3,2,1,0:T(8,128)(2,1)} %get-tuple-element.79), calls=%async_computation.6 | async-start | bytes 1703936 | tf_op jit(solution)/shard_map/all_to_all | solution.py:442
  132.0 105.8 %all-to-all-start.7 = ((bf16[8,2,104,512]{3,2,1,0:T(8,128)(2,1)}), bf16[8,2,104,512]{3,2,1,0:T(8,128)(2,1)}, u32[]{:S(2)}, u32[]{:S(2)}) async-start(bf16[8,2,104,512]{3,2,1,0:T(8,128)(2,1)} %get-tuple-element.85), calls=%async_computation.7 | async-start | bytes 3407872 | tf_op jit(solution)/shard_map/all_to_all | solution.py:442
  137.6 15.6 %collective-permute-start.2 = (bf16[64,512]{1,0:T(8,128)(2,1)S(1)}, bf16[64,512]{1,0:T(8,128)(2,1)S(1)}, u32[]{:S(2)}, u32[]{:S(2)}) collective-permute-start(bf16[64,512]{1,0:T(8,128)(2,1)S(1)} %slice_bitcast_fusion.refs_6_.r0), channel_id=1, source_target_pairs={{0,192},{32,224},{64,0},{96,32},{128,64},{160,96},{192,128},{224,1... | collective-permute-start | bytes 196616 | tf_op jit(solution)/shard_map/ppermute | solution.py:498
  137.7 15.5 %collective-permute-start.1 = (bf16[64,512]{1,0:T(8,128)(2,1)S(1)}, bf16[64,512]{1,0:T(8,128)(2,1)S(1)}, u32[]{:S(2)}, u32[]{:S(2)}) collective-permute-start(bf16[64,512]{1,0:T(8,128)(2,1)S(1)} %slice_bitcast_fusion.refs_6_.r0), channel_id=1, source_target_pairs={{0,128},{32,160},{64,192},{96,224},{128,0},{160,32},{192,64},{224,... | collective-permute-start | bytes 196616 | tf_op jit(solution)/shard_map/ppermute | solution.py:498
  145.5 7.7 %collective-permute-start = (bf16[64,512]{1,0:T(8,128)(2,1)S(1)}, bf16[64,512]{1,0:T(8,128)(2,1)S(1)}, u32[]{:S(2)}, u32[]{:S(2)}) collective-permute-start(bf16[64,512]{1,0:T(8,128)(2,1)S(1)} %slice_bitcast_fusion.refs_6_.r0), channel_id=1, source_target_pairs={{0,64},{32,96},{64,128},{96,160},{128,192},{160,224},{192,0},{224,... | collective-permute-start | bytes 196616 | tf_op jit(solution)/shard_map/ppermute | solution.py:498
  153.6 14.2 %collective-permute-start.5 = (bf16[64,512]{1,0:T(8,128)(2,1)S(1)}, bf16[64,512]{1,0:T(8,128)(2,1)S(1)}, u32[]{:S(2)}, u32[]{:S(2)}) collective-permute-start(bf16[64,512]{1,0:T(8,128)(2,1)S(1)} %get-tuple-element.59.refs_7_.r0), channel_id=1, source_target_pairs={{0,192},{32,224},{64,0},{96,32},{128,64},{160,96},{192,128},{224,1... | collective-permute-start | bytes 196616 | tf_op jit(solution)/shard_map/ppermute | solution.py:498
  155.7 12.2 %collective-permute-start.4 = (bf16[64,512]{1,0:T(8,128)(2,1)S(1)}, bf16[64,512]{1,0:T(8,128)(2,1)S(1)}, u32[]{:S(2)}, u32[]{:S(2)}) collective-permute-start(bf16[64,512]{1,0:T(8,128)(2,1)S(1)} %get-tuple-element.59.refs_7_.r0), channel_id=1, source_target_pairs={{0,128},{32,160},{64,192},{96,224},{128,0},{160,32},{192,64},{224,... | collective-permute-start | bytes 196616 | tf_op jit(solution)/shard_map/ppermute | solution.py:498
  170.2 9.3 %collective-permute-start.8 = (bf16[64,512]{1,0:T(8,128)(2,1)S(1)}, bf16[64,512]{1,0:T(8,128)(2,1)S(1)}, u32[]{:S(2)}, u32[]{:S(2)}) collective-permute-start(bf16[64,512]{1,0:T(8,128)(2,1)S(1)} %get-tuple-element.65.refs_7_.r0), channel_id=1, source_target_pairs={{0,192},{32,224},{64,0},{96,32},{128,64},{160,96},{192,128},{224,1... | collective-permute-start | bytes 196616 | tf_op jit(solution)/shard_map/ppermute | solution.py:498
  172.8 8.2 %collective-permute-start.7 = (bf16[64,512]{1,0:T(8,128)(2,1)S(1)}, bf16[64,512]{1,0:T(8,128)(2,1)S(1)}, u32[]{:S(2)}, u32[]{:S(2)}) collective-permute-start(bf16[64,512]{1,0:T(8,128)(2,1)S(1)} %get-tuple-element.65.refs_7_.r0), channel_id=1, source_target_pairs={{0,128},{32,160},{64,192},{96,224},{128,0},{160,32},{192,64},{224,... | collective-permute-start | bytes 196616 | tf_op jit(solution)/shard_map/ppermute | solution.py:498
  174.6 6.4 %collective-permute-start.6 = (bf16[64,512]{1,0:T(8,128)(2,1)S(1)}, bf16[64,512]{1,0:T(8,128)(2,1)S(1)}, u32[]{:S(2)}, u32[]{:S(2)}) collective-permute-start(bf16[64,512]{1,0:T(8,128)(2,1)S(1)} %get-tuple-element.65.refs_7_.r0), channel_id=1, source_target_pairs={{0,64},{32,96},{64,128},{96,160},{128,192},{160,224},{192,0},{224,... | collective-permute-start | bytes 196616 | tf_op jit(solution)/shard_map/ppermute | solution.py:498
  182.3 9.8 %collective-permute-start.11 = (bf16[64,512]{1,0:T(8,128)(2,1)S(1)}, bf16[64,512]{1,0:T(8,128)(2,1)S(1)}, u32[]{:S(2)}, u32[]{:S(2)}) collective-permute-start(bf16[64,512]{1,0:T(8,128)(2,1)S(1)} %get-tuple-element.71.refs_7_.r0), channel_id=1, source_target_pairs={{0,192},{32,224},{64,0},{96,32},{128,64},{160,96},{192,128},{224,1... | collective-permute-start | bytes 196616 | tf_op jit(solution)/shard_map/ppermute | solution.py:498
  184.1 8.1 %collective-permute-start.10 = (bf16[64,512]{1,0:T(8,128)(2,1)S(1)}, bf16[64,512]{1,0:T(8,128)(2,1)S(1)}, u32[]{:S(2)}, u32[]{:S(2)}) collective-permute-start(bf16[64,512]{1,0:T(8,128)(2,1)S(1)} %get-tuple-element.71.refs_7_.r0), channel_id=1, source_target_pairs={{0,128},{32,160},{64,192},{96,224},{128,0},{160,32},{192,64},{224,... | collective-permute-start | bytes 196616 | tf_op jit(solution)/shard_map/ppermute | solution.py:498
  194.2 10.1 %collective-permute-start.14 = (bf16[64,512]{1,0:T(8,128)(2,1)S(1)}, bf16[64,512]{1,0:T(8,128)(2,1)S(1)}, u32[]{:S(2)}, u32[]{:S(2)}) collective-permute-start(bf16[64,512]{1,0:T(8,128)(2,1)S(1)} %get-tuple-element.77.refs_7_.r0), channel_id=1, source_target_pairs={{0,192},{32,224},{64,0},{96,32},{128,64},{160,96},{192,128},{224,1... | collective-permute-start | bytes 196616 | tf_op jit(solution)/shard_map/ppermute | solution.py:498
  197.1 8.4 %collective-permute-start.13 = (bf16[64,512]{1,0:T(8,128)(2,1)S(1)}, bf16[64,512]{1,0:T(8,128)(2,1)S(1)}, u32[]{:S(2)}, u32[]{:S(2)}) collective-permute-start(bf16[64,512]{1,0:T(8,128)(2,1)S(1)} %get-tuple-element.77.refs_7_.r0), channel_id=1, source_target_pairs={{0,128},{32,160},{64,192},{96,224},{128,0},{160,32},{192,64},{224,... | collective-permute-start | bytes 196616 | tf_op jit(solution)/shard_map/ppermute | solution.py:498
  198.9 6.6 %collective-permute-start.12 = (bf16[64,512]{1,0:T(8,128)(2,1)S(1)}, bf16[64,512]{1,0:T(8,128)(2,1)S(1)}, u32[]{:S(2)}, u32[]{:S(2)}) collective-permute-start(bf16[64,512]{1,0:T(8,128)(2,1)S(1)} %get-tuple-element.77.refs_7_.r0), channel_id=1, source_target_pairs={{0,64},{32,96},{64,128},{96,160},{128,192},{160,224},{192,0},{224,... | collective-permute-start | bytes 196616 | tf_op jit(solution)/shard_map/ppermute | solution.py:498
  206.8 9.6 %collective-permute-start.17 = (bf16[64,512]{1,0:T(8,128)(2,1)S(1)}, bf16[64,512]{1,0:T(8,128)(2,1)S(1)}, u32[]{:S(2)}, u32[]{:S(2)}) collective-permute-start(bf16[64,512]{1,0:T(8,128)(2,1)S(1)} %get-tuple-element.83.refs_7_.r0), channel_id=1, source_target_pairs={{0,192},{32,224},{64,0},{96,32},{128,64},{160,96},{192,128},{224,1... | collective-permute-start | bytes 196616 | tf_op jit(solution)/shard_map/ppermute | solution.py:498
  208.5 8.0 %collective-permute-start.16 = (bf16[64,512]{1,0:T(8,128)(2,1)S(1)}, bf16[64,512]{1,0:T(8,128)(2,1)S(1)}, u32[]{:S(2)}, u32[]{:S(2)}) collective-permute-start(bf16[64,512]{1,0:T(8,128)(2,1)S(1)} %get-tuple-element.83.refs_7_.r0), channel_id=1, source_target_pairs={{0,128},{32,160},{64,192},{96,224},{128,0},{160,32},{192,64},{224,... | collective-permute-start | bytes 196616 | tf_op jit(solution)/shard_map/ppermute | solution.py:498
  218.5 10.6 %collective-permute-start.20 = (bf16[64,512]{1,0:T(8,128)(2,1)S(1)}, bf16[64,512]{1,0:T(8,128)(2,1)S(1)}, u32[]{:S(2)}, u32[]{:S(2)}) collective-permute-start(bf16[64,512]{1,0:T(8,128)(2,1)S(1)} %get-tuple-element.89.refs_7_.r0), channel_id=1, source_target_pairs={{0,192},{32,224},{64,0},{96,32},{128,64},{160,96},{192,128},{224,1... | collective-permute-start | bytes 196616 | tf_op jit(solution)/shard_map/ppermute | solution.py:498
  221.4 8.2 %collective-permute-start.19 = (bf16[64,512]{1,0:T(8,128)(2,1)S(1)}, bf16[64,512]{1,0:T(8,128)(2,1)S(1)}, u32[]{:S(2)}, u32[]{:S(2)}) collective-permute-start(bf16[64,512]{1,0:T(8,128)(2,1)S(1)} %get-tuple-element.89.refs_7_.r0), channel_id=1, source_target_pairs={{0,128},{32,160},{64,192},{96,224},{128,0},{160,32},{192,64},{224,... | collective-permute-start | bytes 196616 | tf_op jit(solution)/shard_map/ppermute | solution.py:498
  223.5 6.6 %collective-permute-start.18 = (bf16[64,512]{1,0:T(8,128)(2,1)S(1)}, bf16[64,512]{1,0:T(8,128)(2,1)S(1)}, u32[]{:S(2)}, u32[]{:S(2)}) collective-permute-start(bf16[64,512]{1,0:T(8,128)(2,1)S(1)} %get-tuple-element.89.refs_7_.r0), channel_id=1, source_target_pairs={{0,64},{32,96},{64,128},{96,160},{128,192},{160,224},{192,0},{224,... | collective-permute-start | bytes 196616 | tf_op jit(solution)/shard_map/ppermute | solution.py:498
  232.0 10.2 %collective-permute-start.23 = (bf16[64,512]{1,0:T(8,128)(2,1)S(1)}, bf16[64,512]{1,0:T(8,128)(2,1)S(1)}, u32[]{:S(2)}, u32[]{:S(2)}) collective-permute-start(bf16[64,512]{1,0:T(8,128)(2,1)S(1)} %get-tuple-element.94.r0), channel_id=1, source_target_pairs={{0,192},{32,224},{64,0},{96,32},{128,64},{160,96},{192,128},{224,1... | collective-permute-start | bytes 196616 | tf_op jit(solution)/shard_map/ppermute | solution.py:498
  233.6 8.6 %collective-permute-start.22 = (bf16[64,512]{1,0:T(8,128)(2,1)S(1)}, bf16[64,512]{1,0:T(8,128)(2,1)S(1)}, u32[]{:S(2)}, u32[]{:S(2)}) collective-permute-start(bf16[64,512]{1,0:T(8,128)(2,1)S(1)} %get-tuple-element.94.r0), channel_id=1, source_target_pairs={{0,128},{32,160},{64,192},{96,224},{128,0},{160,32},{192,64},{224,... | collective-permute-start | bytes 196616 | tf_op jit(solution)/shard_map/ppermute | solution.py:498
  247.8 21.9 %all-to-all-start.8 = ((bf16[32,2,56,128]{3,2,1,0:T(8,128)(2,1)}), bf16[32,2,56,128]{3,2,1,0:T(8,128)(2,1)S(1)}, u32[]{:S(2)}, u32[]{:S(2)}) async-start(bf16[32,2,56,128]{3,2,1,0:T(8,128)(2,1)} %bitcast.12), calls=%async_computation.8 | async-start | bytes 1835008 | tf_op jit(solution)/shard_map/all_to_all | solution.py:442
  269.8 16.5 %collective-permute-start.24 = (bf16[32,56,128]{2,1,0:T(8,128)(2,1)S(1)}, bf16[32,56,128]{2,1,0:T(8,128)(2,1)S(1)}, u32[]{:S(2)}, u32[]{:S(2)}) collective-permute-start(bf16[32,56,128]{2,1,0:T(8,128)(2,1)S(1)} %get-tuple-element.95), channel_id=1, source_target_pairs={{0,1},{1,0},{2,3},{3,2},{4,5},{5,4},{6,7},{7,6},{8,9},{9,8},{10,11... | collective-permute-start | bytes 1376264 | tf_op jit(solution)/shard_map/ppermute | solution.py:520
  (66 other events, 593.2 us)
